TPU v7x, 256 devices: a whole 4x4x8 slice. The times are simulated.
256 devices in a mesh: tm: 32 (over x, y, core), cell: 8 (over z).
Axes of the slice: x: 4, y: 4, z: 8, core: 2. Of those that a mesh axis runs over, the one named last changes fastest.
Arguments:
- anomalies: bfloat16 [96, 2, 16384, 256], P('tm', None, 'cell'), may hold values from -6 to 6
- obs_cells: int32 [96, 256], P('tm', 'cell'), may hold values from 0 to 16383, as said below
- obs_counts: int32 [96, 8], P('tm', 'cell'), may hold values from 16 to 32
- obs_precision: float32 [96, 256], P('tm', 'cell'), may hold values from 0.1 to 1
- inflation: float32 [96], P('tm'), may hold values from 1 to 1.12
Outputs:
- smoothed: bfloat16 [96, 2, 16384, 256], P('tm', None, 'cell')
Inputs may be any that keep to these rules, and one draw needn't show every extreme that they name: `obs_cells`: slot k of a window names a cell of the block of 2048 cells that starts at (k // 32) * 2048; two slots may name the same cell.
All inputs are finite; a program needn't handle non-finite values.
Results may differ from a plain program's by a relative error of at most 0.017.
Values may be sent and summed in bfloat16 or wider, within the bound.
No kernel may reach another device: no remote copies, remote signals or barrier semaphores. Data moves between devices by JAX's collectives and lax.ppermute only.
A program may use at most 128 MiB of HBM per device.

v0:
```python
import jax
import jax.numpy as jnp
from jax import lax
from jax.sharding import Mesh
from jax.sharding import PartitionSpec as P

TM = ("tm_0", "tm_1", "tm_2")


def copy_for_each(array, axis):
    copies = jnp.broadcast_to(array, (lax.axis_size(axis), *array.shape))
    return lax.all_to_all(copies, axis, split_axis=0, concat_axis=0, tiled=True)


def joined_along(parts, dim):
    parts = jnp.moveaxis(parts, 0, dim)
    shape = parts.shape
    return parts.reshape(*shape[:dim], shape[dim] * shape[dim + 1], *shape[dim + 2 :])


def gathered_copies(array, axis, dim):
    parts = copy_for_each(array, axis)
    return joined_along(parts, dim)


def nothing_yet(array, identity):
    return jnp.zeros_like(array) + jnp.asarray(identity, array.dtype)


def carried_in(array, axes, combine, identity):
    before = start = nothing_yet(array, identity)
    running = array
    for axis in reversed(axes):
        count, mine = (lax.axis_size(axis), lax.axis_index(axis))
        pieces = lax.all_gather(running.astype(jnp.bfloat16), axis)
        inside, running = (start, start)
        for k in reversed(range(count)):
            passed = k > mine
            running = combine(running, pieces[k].astype(array.dtype))
            inside = jnp.where(passed, running, inside)
        before = combine(inside, before)
    return before


def matmul_f32(left, right):
    return jnp.dot(left, right, precision=lax.Precision.HIGHEST, preferred_element_type=jnp.float32)


def gram_of(picked, weights):
    as_float = picked.astype(jnp.float32)
    weighted = as_float * weights[:, :, None]
    return jnp.einsum(
        "wkm,wkn->wmn",
        weighted,
        as_float,
        precision=lax.Precision.HIGHEST,
        preferred_element_type=jnp.float32,
    )


def transform_of(gram, rho):
    members = gram.shape[-1]
    unit_matrix = jnp.eye(members, dtype=jnp.float32)
    factor = jnp.linalg.cholesky((members - 1.0) * unit_matrix[None] + gram)
    inverse = jax.vmap(
        lambda lower_f: jax.scipy.linalg.solve_triangular(lower_f, unit_matrix, lower=True)
    )(factor)
    scale = rho * jnp.sqrt(jnp.float32(members - 1.0))
    return scale[:, None, None] * jnp.swapaxes(inverse, 1, 2)


def local(anomalies, obs_cells, obs_counts, obs_precision, inflation):
    cell_width = anomalies.shape[2]
    members = anomalies.shape[3]
    slots = obs_cells.shape[1]
    first_cell = lax.axis_index("cell") * cell_width
    offsets = obs_cells - first_cell
    picked = jax.vmap(lambda field, where_at: field[0][where_at])(anomalies, offsets)
    live = jnp.arange(slots, dtype=jnp.int32)[None, :] < obs_counts
    picked = jnp.where(live[:, :, None], picked, jnp.zeros_like(picked))
    weights = jnp.where(live, obs_precision, jnp.float32(0.0))
    gathered, gathered_weights = (
        gathered_copies(picked, "cell", 1),
        gathered_copies(weights.astype(jnp.bfloat16), "cell", 1).astype(weights.dtype),
    )
    gram = gram_of(gathered, gathered_weights)
    transforms = transform_of(gram, inflation)
    windows = transforms.shape[0]
    partial_list = [transforms[windows - 1]]
    for window in range(windows - 2, -1, -1):
        partial_list.insert(0, matmul_f32(transforms[window], partial_list[0]))
    own_product = partial_list[0]
    unit_matrix = jnp.eye(members, dtype=jnp.float32)
    later_product = carried_in(
        own_product, TM, lambda earlier, latter: matmul_f32(latter, earlier), unit_matrix
    )
    suffixes = jnp.stack(
        [matmul_f32(partial_value, later_product) for partial_value in partial_list]
    )
    weight_mats = suffixes.astype(jnp.bfloat16)
    flat = anomalies.reshape(windows, 2 * cell_width, members)
    result = jnp.einsum("wcm,wmn->wcn", flat, weight_mats, preferred_element_type=jnp.float32)
    return result.astype(jnp.bfloat16).reshape(anomalies.shape)


def solution(mesh):
    torus = Mesh(
        mesh.devices.reshape(4, 4, 2, mesh.shape["cell"]), ("tm_0", "tm_1", "tm_2", "cell")
    )
    return jax.shard_map(
        local,
        mesh=torus,
        in_specs=(P(TM, None, "cell", None), P(TM, "cell"), P(TM, "cell"), P(TM, "cell"), P(TM)),
        out_specs=P(TM, None, "cell", None),
        check_vma=False,
    )
```

profile of v0, /device:TPU:6, one launch (start us, length us, event | category | flops | bytes accessed | tf_op | source)
XLA Modules:
  0.0 254.6 jit_solution(16224712677104339042)
XLA Ops:
  0.0 0.8 select_convert_fusion
  0.8 0.6 broadcast_in_dim.44
  1.4 8.5 %all-to-all-start.1 = ((bf16[8,3,32]{2,1,0:T(4,128)(2,1)}), bf16[8,3,32]{2,1,0:T(4,128)(2,1)S(1)}, u32[]{:S(2)}, u32[]{:S(2)}) async-start(bf16[8,3,32]{2,1,0:T(4,128)(2,1)} %broadcast_in_dim.44), calls=%async_computation.1 | async-start | bytes 16384 | tf_op jit(solution)/shard_map/all_to_all | solution.py:12
  9.8 0.7 iota_compare_fusion.10
  10.6 0.8 fusion.32
  11.5 0.7 fusion.66
  12.1 0.1 reshape.98
  12.2 2.1 slice_bitcast_fusion
  14.3 1.5 gather_fusion
  15.8 0.1 broadcast_select_fusion
  15.9 1.6 all-to-all-done.1
  17.6 0.8 broadcast_in_dim.42
  18.3 5.6 %all-to-all-start = ((bf16[8,3,32,256]{3,2,1,0:T(8,128)(2,1)}), bf16[8,3,32,256]{3,2,1,0:T(8,128)(2,1)S(1)}, u32[]{:S(2)}, u32[]{:S(2)}) async-start(bf16[8,3,32,256]{3,2,1,0:T(8,128)(2,1)} %broadcast_in_dim.42), calls=%async_computation | async-start | bytes 786432 | tf_op jit(solution)/shard_map/all_to_all | solution.py:12
  24.0 0.7 broadcast_multiply_fusion
  24.7 0.1 reshape.97
  24.7 13.3 %all-to-all-done = bf16[8,3,32,256]{3,2,1,0:T(8,128)(2,1)S(1)} async-done(((bf16[8,3,32,256]{3,2,1,0:T(8,128)(2,1)}), bf16[8,3,32,256]{3,2,1,0:T(8,128)(2,1)S(1)}, u32[]{:S(2)}, u32[]{:S(2)}) %all-to-all-start) | async-done | bytes 393248 | tf_op jit(solution)/shard_map/all_to_all | solution.py:12
  38.1 1.0 fusion.7
  39.0 0.3 copy.53
  39.3 1.2 fusion.6
  40.5 35.2 %custom-call.17 = f32[3,128,128]{2,1,0:T(8,128)S(1)} custom-call(f32[3,128,128]{2,1,0:T(8,128)S(1)} %cholesky.122), custom_call_target="Cholesky" | custom-call | tf_op jit(solution)/shard_map/jit(cholesky)/cholesky | solution.py:64
  75.7 29.5 %custom-call.18 = f32[3,1,128,128]{2,3,1,0:T(8,128)S(1)} custom-call(f32[3,1,128,128]{3,2,1,0:T(8,128)S(1)} %select_bitcast_fusion), custom_call_target="InvertDiagBlocksLowerTriangular" | custom-call | tf_op jit(solution)/shard_map/jit(cholesky)/cholesky | solution.py:64
  105.2 0.1 cholesky.117
  105.3 0.4 constant_dynamic-update-slice_fusion.1
  105.6 0.5 convolution_subtract_fusion.1
  106.2 35.2 %custom-call.19 = f32[3,128,128]{2,1,0:T(8,128)S(1)} custom-call(f32[3,128,128]{2,1,0:T(8,128)S(1)} %convolution_subtract_fusion.1), custom_call_target="Cholesky" | custom-call | tf_op jit(solution)/shard_map/jit(cholesky)/cholesky | solution.py:64
  141.4 0.1 compare_reduce_fusion
  141.5 0.1 compare_reduce_fusion.1
  141.6 0.2 select_select_fusion
  141.8 0.1 triangular_solve.86
  141.9 4.0 %while.1 = (s32[]{:T(128)}, f32[3,256,256]{2,1,0:T(8,128)S(1)}, s32[2,2]{1,0:T(2,128)S(1)}, f32[2,3,128,128]{3,2,0,1:T(8,128)S(1)}, s32[]{:T(128)}) while((s32[]{:T(128)}, f32[3,256,256]{2,1,0:T(8,128)S(1)}, s32[2,2]{1,0:T(2,128)S(1)}, f32[2,3,128,128]{3,2,0,1:T(8,128)S(1)}, s32[]{:T(128)}) %tuple.27), condition=%wide.while_cond, body=%wide.while_body.sunk | while | flops 2 | bytes 393333 | solution.py:66
  142.0 0.6 fusion.97
  142.6 1.3 bitcast_dynamic-update-slice_fusion.2
  144.0 0.6 fusion.97
  144.6 1.3 bitcast_dynamic-update-slice_fusion.2
  145.9 59.0 %custom-call.20 = f32[3,2,128,128]{2,3,1,0:T(8,128)S(1)} custom-call(f32[3,2,128,128]{3,2,1,0:T(8,128)S(1)} %bitcast.104), custom_call_target="InvertDiagBlocksLowerTriangular" | custom-call | tf_op jit(solution)/shard_map/vmap(jit(_solve_triangular))/triangular_solve | solution.py:66
  204.9 0.5 fusion.36
  205.4 0.5 convolution_subtract_fusion
  205.9 0.5 fusion.35
  206.4 0.1 fusion.4
  206.6 0.6 fusion.26
  207.2 0.0 slice-start
  207.2 0.6 fusion.70
  207.8 2.1 all-gather
  209.9 0.2 fusion.30
  210.1 0.3 fusion.71
  210.4 13.3 %all-gather.1 = bf16[1024,256]{1,0:T(8,128)(2,1)S(1)} all-gather(bf16[256,256]{1,0:T(8,128)(2,1)S(1)} %get-tuple-element.32), channel_id=3, replica_groups=mesh['tm_0'=4,'tm_1'=4,'tm_2'=2,'cell'=8] {'tm_1'}, dimensions={0}, use_global_device_ids=true | all-gather | bytes 655360 | tf_op jit(solution)/shard_map/all_gather | solution.py:35
  223.7 0.2 fusion.29
  223.9 0.3 fusion.48
  224.3 0.3 fusion.50
  224.6 0.3 fusion.72
  224.9 12.8 %all-gather.2 = bf16[1024,256]{1,0:T(8,128)(2,1)S(1)} all-gather(bf16[256,256]{1,0:T(8,128)(2,1)S(1)} %get-tuple-element.34), channel_id=4, replica_groups=mesh['tm_0'=4,'tm_1'=4,'tm_2'=2,'cell'=8] {'tm_0'}, dimensions={0}, use_global_device_ids=true | all-gather | bytes 655360 | tf_op jit(solution)/shard_map/all_gather | solution.py:35
  237.7 0.2 fusion.28
  237.9 0.0 slice-start.1
  237.9 0.3 fusion.42
  238.2 0.3 fusion.44
  238.5 0.3 fusion.17
  238.8 0.3 convolution_select_fusion
  239.2 0.4 fusion.22
  239.6 0.4 fusion.73
  240.0 0.6 fusion.3
  240.6 0.4 fusion.2
  241.0 0.4 fusion.1
  241.4 4.6 %fusion = bf16[3,4096,256]{1,2,0:T(8,128)(2,1)} fusion(bf16[3,4096,256]{2,1,0:T(8,128)(2,1)S(1)} %bitcast.98, bf16[1,256,256]{2,1,0:T(8,128)(2,1)S(1)} %fusion.3, bf16[1,256,256]{2,1,0:T(8,128)(2,1)S(1)} %fusion.2, bf16[1,256,256]{2,1,0:T(8,128)(2,1)S(1)} %fusion.1), kind=kOutput, calls=%fused_computation.4 | convolution fusion | flops 1614151680 | bytes 12976128 | tf_op jit(solution)/shard_map/wcm,wmn->wcn/dot_general | solution.py:102
  246.0 8.6 %copy.66 = bf16[3,4096,256]{2,1,0:T(8,128)(2,1)} copy(bf16[3,4096,256]{1,2,0:T(8,128)(2,1)} %fusion) | data formatting | bytes 12582912 | tf_op jit(solution)/shard_map/reshape | solution.py:103
  (19 shorter events, 0.2 us)
Async XLA Ops:
  1.4 16.2 %all-to-all-start.1 = ((bf16[8,3,32]{2,1,0:T(4,128)(2,1)}), bf16[8,3,32]{2,1,0:T(4,128)(2,1)S(1)}, u32[]{:S(2)}, u32[]{:S(2)}) async-start(bf16[8,3,32]{2,1,0:T(4,128)(2,1)} %broadcast_in_dim.44), calls=%async_computation.1 | async-start | bytes 16384 | tf_op jit(solution)/shard_map/all_to_all | solution.py:12
  18.3 19.7 %all-to-all-start = ((bf16[8,3,32,256]{3,2,1,0:T(8,128)(2,1)}), bf16[8,3,32,256]{3,2,1,0:T(8,128)(2,1)S(1)}, u32[]{:S(2)}, u32[]{:S(2)}) async-start(bf16[8,3,32,256]{3,2,1,0:T(8,128)(2,1)} %broadcast_in_dim.42), calls=%async_computation | async-start | bytes 786432 | tf_op jit(solution)/shard_map/all_to_all | solution.py:12
  207.2 34.2 %slice-start = ((s8[6291456]{0:T(1024)(128)(4,1)}), s8[4194304]{0:T(1024)(128)(4,1)S(1)}, s32[]{:S(2)}) async-start(s8[6291456]{0:T(1024)(128)(4,1)} %bitcast.96), calls=%async_computation.2 | async-start | bytes 8388608
  237.9 3.5 %slice-start.1 = ((s8[6291456]{0:T(1024)(128)(4,1)}), s8[2097152]{0:T(1024)(128)(4,1)S(1)}, s32[]{:S(2)}) async-start(s8[6291456]{0:T(1024)(128)(4,1)} %bitcast.96), calls=%async_computation.3 | async-start | bytes 4194304
where the time goes:
time: 256 us; the launch traced here: 255 us
  other arithmetic  164 us (64%)
  blocking collectives  28.2 us (11%)
  local copies, waits for them, and re-layouts  18 us (7%)
  waiting for transfers between devices  14.9 us (6%)
  matrix products  14.3 us (6%)
  starting transfers between devices  14 us (5%)
    another operation x10, other arithmetic, transform_of(): factor = jnp.linalg.cholesky((members - 1.0) * unit_matrix[None] + gram)  100 us
    another operation x4, other arithmetic, transform_of(): jax.scipy.linalg.solve_triangular(lower_f, unit_matrix, lower=True)  59.2 us
    all_gather x3, blocking collectives, carried_in(): pieces = lax.all_gather(running.astype(jnp.bfloat16), axis)  28.2 us
    all_to_all x2, waiting for transfers between devices, copy_for_each(): return lax.all_to_all(copies, axis, split_axis=0, concat_axis=0, tiled=True)  14.9 us
    all_to_all x2, starting transfers between devices, copy_for_each(): return lax.all_to_all(copies, axis, split_axis=0, concat_axis=0, tiled=True)  14 us
    reshape x1, local copies, waits for them, and re-layouts, local(): return result.astype(jnp.bfloat16).reshape(anomalies.shape)  8.6 us
    dot_general x18, matrix products, matmul_f32(): jnp.dot(left, right, precision=lax.Precision.HIGHEST, preferred_element_t...  6.41 us
  transfers between devices with their start and end apart: 2, of which 2 were waited for; matrix products, arithmetic and copies ran while one was open for 3% of the time, Pallas kernels for 0%

commit v1 on v0

v1 whole, which is shorter than its diff:
```python
import functools
import math
import jax
import jax.numpy as jnp
from jax import lax
from jax.experimental import pallas as pl
from jax.experimental.pallas import tpu as pltpu
from jax.sharding import Mesh
from jax.sharding import PartitionSpec as P

TM = ("tm_0", "tm_1", "tm_2")
VMEM = pltpu.VMEM
F32 = jnp.float32
BF16 = jnp.bfloat16
HI = lax.Precision.HIGHEST
B = 32
T = 8


def dot(a, b, precision=None):
    return jnp.dot(a, b, precision=precision, preferred_element_type=F32)


def dot_nt(a, b, precision=None):
    return lax.dot_general(a, b, (((1,), (1,)), ((), ())), precision=precision, preferred_element_type=F32)


def dot_tn(a, b, precision=None):
    return lax.dot_general(a, b, (((0,), (0,)), ((), ())), precision=precision, preferred_element_type=F32)


def split3(v):
    hi = v.astype(BF16)
    rest = v - hi.astype(F32)
    mid = rest.astype(BF16)
    lo = (rest - mid.astype(F32)).astype(BF16)
    return hi, mid, lo


def dot_x3(a, b):
    ah = a.astype(BF16)
    al = (a - ah.astype(F32)).astype(BF16)
    bh = b.astype(BF16)
    bl = (b - bh.astype(F32)).astype(BF16)
    return dot(ah, bh) + (dot(ah, bl) + dot(al, bh))


def row_of(tile, i):
    return jnp.broadcast_to(tile[i : i + 1, :], tile.shape)


def inverse_factors(tiles, lane):
    n = len(tiles)
    sub = lax.broadcasted_iota(jnp.int32, (T, 128), 0)
    base = (lane // B) * B
    local = lane - base
    roots = []
    for t in range(n):
        cols = []
        for i in range(T):
            index = base + (t * T + i)
            cols.append([jnp.take_along_axis(tiles[r], index, axis=1) if r >= t else None for r in range(n)])
        pivots = []
        for i in range(T):
            j = t * T + i
            pivot = row_of(cols[i][t], i)
            inv = 1.0 / pivot
            pivots.append(pivot)
            here = local == j
            row = jnp.where(here, 1.0, row_of(tiles[t], i)) * inv
            follow = [row_of(cols[m][t], i) * inv for m in range(i + 1, T)]
            for r in range(t, n):
                c = cols[i][r]
                if r == t:
                    c = jnp.where(sub > i, c, 0.0)
                    keep = jnp.where(here & (sub > i), 0.0, tiles[r])
                    keep = jnp.where(here & (sub == i), 1.0, keep)
                else:
                    keep = jnp.where(here, 0.0, tiles[r])
                tiles[r] = keep - c * row
                for m in range(i + 1, T):
                    cols[m][r] = cols[m][r] - c * follow[m - i - 1]
        d = pivots[0]
        for i in range(1, T):
            d = jnp.where(sub == i, pivots[i], d)
        roots.append(lax.rsqrt(d))
    out = []
    for t in range(n):
        low = local <= (sub + t * T)
        out.append(jnp.where(low, tiles[t] * roots[t], 0.0))
    return out


def factor_body(nwin, gram_of_window, X):
    nb = 256 // B
    lane = lax.broadcasted_iota(jnp.int32, (T, 128), 1)
    lane_b = lax.broadcasted_iota(jnp.int32, (B, 128), 1)
    lane_r = lax.broadcasted_iota(jnp.int32, (B, 256), 1)
    rows_b = lax.broadcasted_iota(jnp.int32, (B, 256), 0)
    for w in range(nwin):
        g = gram_of_window(w)
        for k in range(nb):
            X[k, w * B : (w + 1) * B, :] = g[k * B : (k + 1) * B, :] + jnp.where(lane_r == rows_b + k * B, 255.0, 0.0)
    for k in range(nb):
        half = (k * B) // 128
        at = (k * B) % 128
        tiles = []
        for t in range(B // T):
            tile = None
            for w in range(nwin):
                part = X[k, w * B + t * T : w * B + (t + 1) * T, half * 128 : half * 128 + 128]
                shift = (w * B - at) % 128
                if shift:
                    part = pltpu.roll(part, shift, 1)
                tile = part if w == 0 else jnp.where(lane >= w * B, part, tile)
            tiles.append(tile)
        inv = jnp.concatenate(inverse_factors(tiles, lane), axis=0)
        diag = jnp.concatenate([jnp.where(lane_b // B == w, inv, 0.0) for w in range(nwin)], axis=0)
        rows = X[k]
        q = dot(diag[:, : nwin * B], rows, HI)
        lane_q = lax.broadcasted_iota(jnp.int32, (B, 256), 1)
        inside = (lane_q >= k * B) & (lane_q < (k + 1) * B)
        qs = []
        for w in range(nwin):
            shift = (at - w * B) % 128
            moved = jnp.where(lane_b // B == w, inv, 0.0)
            if shift:
                moved = pltpu.roll(moved, shift, 1)
            zero = jnp.zeros((B, 128), F32)
            wide = jnp.concatenate([moved, zero] if half == 0 else [zero, moved], axis=1)
            qw = jnp.where(inside, wide, q[w * B : (w + 1) * B])
            qs.append((qw, moved))
            X[k, w * B : (w + 1) * B, :] = jnp.where(lane_q < (k + 1) * B, qw, 0.0)
        for w in range(nwin):
            qw, moved = qs[w]
            if k + 1 == nb:
                continue
            below = X[k + 1 :, w * B : (w + 1) * B, :]
            nrow = (nb - k - 1) * B
            p = dot_nt(below[:, :, half * 128 : half * 128 + 128].reshape(nrow, 128), moved, HI)
            upd = dot(p, qw, HI).reshape(nb - k - 1, B, 256)
            X[k + 1 :, w * B : (w + 1) * B, :] = jnp.where(inside[None], 0.0, below) - upd


def factor_kernel(g_ref, scale_ref, part_ref, own_ref, X, Y):
    nz = g_ref.shape[0]
    nwin = scale_ref.shape[0]
    slots = 32
    packed = []
    for z in range(nz):
        both = g_ref[z, nwin * slots : nwin * slots + 8, :].astype(F32)
        packed.append((both[:, :128] + both[:, 128:]))
    columns = jnp.concatenate(packed, axis=0)
    columns = jnp.concatenate([columns, columns], axis=0).T

    def gram(w):
        parts = []
        for z in range(nz):
            y = g_ref[z, w * slots : (w + 1) * slots, :]
            Y[w, z * slots : (z + 1) * slots, :] = y
            col = columns[:slots, z * 8 + w : z * 8 + w + 1]
            parts.append(y.astype(F32) * col)
        weighted = jnp.concatenate(parts, axis=0)
        hi, mid, lo = split3(weighted)
        y = Y[w].T
        return dot(y, hi) + (dot(y, mid) + dot(y, lo))

    factor_body(nwin, gram, X)
    s = None
    for w in reversed(range(nwin)):
        x = X[:, w * B : (w + 1) * B, :].reshape(256, 256) * scale_ref[w]
        s = x if s is None else dot_x3(s, x)
        part_ref[w] = s
    own_ref[...] = s.astype(BF16)


def factor_call(g, scale):
    nwin = scale.shape[0]
    return pl.pallas_call(
        factor_kernel,
        in_specs=[pl.BlockSpec(memory_space=pltpu.VMEM), pl.BlockSpec(memory_space=pltpu.SMEM)],
        out_specs=[pl.BlockSpec(memory_space=pltpu.VMEM)] * 2,
        out_shape=[jax.ShapeDtypeStruct((nwin, 256, 256), F32), jax.ShapeDtypeStruct((256, 256), BF16)],
        scratch_shapes=[pltpu.VMEM((256 // B, nwin * B, 256), F32), pltpu.VMEM((nwin, 256, 256), BF16)],
        name="factor",
    )(g, scale)


WHOLE = pl.BlockSpec(memory_space=pltpu.VMEM)
SCALARS = pl.BlockSpec(memory_space=pltpu.SMEM)


def pick_kernel(cells_ref, counts_ref, precision_ref, field_ref, out_ref, near, row_scr, sem):
    nwin, slots = cells_ref.shape
    width = field_ref.shape[2]

    def copy_of(w, k):
        offset = lax.rem(cells_ref[w, k], width)
        first = pl.multiple_of((offset // 16) * 16, 16)
        return pltpu.make_async_copy(field_ref.at[w, 0, pl.ds(first, 16), :], near.at[w * slots + k], sem)

    for w in range(nwin):
        for k in range(slots):
            copy_of(w, k).start()
    row_scr[...] = jnp.zeros(row_scr.shape, F32)
    lane = lax.broadcasted_iota(jnp.int32, (1, slots), 1)
    for w in range(nwin):
        row_scr[w : w + 1, :slots] = jnp.where(lane < counts_ref[w, 0], precision_ref[w : w + 1, :], 0.0)
    live = row_scr[...]
    high = live.astype(BF16)
    low = (live - high.astype(F32)).astype(BF16)
    tail = jnp.concatenate([high, low], axis=1)
    pltpu.make_async_copy(near, near, sem).wait()
    sub = lax.broadcasted_iota(jnp.int32, (16, 256), 0)
    rows = []
    for w in range(nwin):
        for k in range(slots):
            within = lax.rem(cells_ref[w, k], 16)
            tile = near[w * slots + k].astype(F32)
            rows.append(jnp.sum(jnp.where(sub == within, tile, 0.0), axis=0, keepdims=True))
    for w in range(nwin):
        block = jnp.concatenate(rows[w * slots : (w + 1) * slots], axis=0).astype(BF16)
        for z in range(out_ref.shape[0]):
            out_ref[z, w * slots : (w + 1) * slots, :] = block
    for z in range(out_ref.shape[0]):
        out_ref[z, nwin * slots :, :] = tail


def pick_call(copies, anomalies, obs_cells, obs_counts, obs_precision):
    nwin, slots = obs_cells.shape
    members = anomalies.shape[3]
    return pl.pallas_call(
        pick_kernel,
        in_specs=[SCALARS, SCALARS, WHOLE, pl.BlockSpec(memory_space=pl.ANY)],
        out_specs=WHOLE,
        out_shape=jax.ShapeDtypeStruct((copies, nwin * slots + 8, members), BF16),
        scratch_shapes=[
            pltpu.VMEM((nwin * slots, 16, members), BF16),
            pltpu.VMEM((8, 128), F32),
            pltpu.SemaphoreType.DMA,
        ],
        name="pick",
    )(obs_cells, obs_counts, obs_precision, anomalies)


def identity_bf16(n):
    return (lax.broadcasted_iota(jnp.int32, (n, n), 0) == lax.broadcasted_iota(jnp.int32, (n, n), 1)).astype(BF16)


def pair_kernel(mine_ref, other_ref, both_ref):
    core = lax.axis_index("tm_2")
    first = jnp.where(core == 0, mine_ref[...].astype(F32), other_ref[...].astype(F32)).astype(BF16)
    second = jnp.where(core == 0, other_ref[...].astype(F32), mine_ref[...].astype(F32)).astype(BF16)
    both_ref[...] = dot(second, first).astype(BF16)


def later_of(q, me):
    return [lambda: dot_x3(dot(q[3], q[2]), q[1].astype(F32)), lambda: dot(q[3], q[2]), lambda: q[3].astype(F32)]


def ring_kernel(p0, p1, p2, p3, total_ref, later_ref, q):
    me = lax.axis_index("tm_1")
    for s, piece in enumerate((p0, p1, p2, p3)):
        q[lax.rem(me + s, 4)] = piece[...]
    high = dot(q[3], q[2])
    total_ref[...] = dot_x3(high, dot(q[1], q[0])).astype(BF16)
    later_ref[...] = high

    @pl.when(me == 0)
    def _():
        later_ref[...] = dot_x3(high, q[1].astype(F32))

    @pl.when(me == 2)
    def _():
        later_ref[...] = q[3].astype(F32)

    @pl.when(me == 3)
    def _():
        later_ref[...] = identity_bf16(256).astype(F32)


def inner_kernel(later_ref, other_ref, part_ref, out_ref, before):
    core = lax.axis_index("tm_2")
    before[...] = later_ref[...]

    @pl.when(core == 0)
    def _():
        before[...] = dot_x3(later_ref[...], other_ref[...].astype(F32))

    for w in range(part_ref.shape[0]):
        out_ref[w] = dot_x3(before[...], part_ref[w])


def apply_kernel(p1, p2, p3, inner_ref, field_ref, out_ref, q, later, weights):
    @pl.when((pl.program_id(0) == 0) & (pl.program_id(1) == 0))
    def _():
        me = lax.axis_index("tm_0")
        for s, piece in enumerate((p1, p2, p3)):
            q[lax.rem(me + s + 1, 4)] = piece[...]

        @pl.when(me == 0)
        def _():
            later[...] = dot_x3(dot(q[3], q[2]), q[1].astype(F32))

        @pl.when(me == 1)
        def _():
            later[...] = dot(q[3], q[2])

        @pl.when(me == 2)
        def _():
            later[...] = q[3].astype(F32)

        @pl.when(me == 3)
        def _():
            later[...] = identity_bf16(256).astype(F32)

        for w in range(inner_ref.shape[0]):
            weights[w] = dot_x3(later[...], inner_ref[w]).astype(BF16)

    out_ref[0] = dot_nt(field_ref[0], weights[pl.program_id(0)]).astype(BF16)


def apply_call(pieces, inner, flat):
    nwin, rows, members = flat.shape
    step = 1024
    block = pl.BlockSpec((1, step, members), lambda w, i: (w, i, 0))
    return pl.pallas_call(
        apply_kernel,
        grid=(nwin, rows // step),
        in_specs=[WHOLE] * 4 + [block],
        out_specs=block,
        out_shape=jax.ShapeDtypeStruct(flat.shape, BF16),
        scratch_shapes=[
            pltpu.VMEM((4, members, members), BF16),
            pltpu.VMEM((members, members), F32),
            pltpu.VMEM((nwin, members, members), BF16),
        ],
        name="apply",
    )(*pieces, inner, flat)


def simple_call(kernel, name, out_shape, scratch, *args):
    return pl.pallas_call(
        kernel,
        in_specs=[WHOLE] * len(args),
        out_specs=jax.tree.map(lambda _: WHOLE, out_shape),
        out_shape=out_shape,
        scratch_shapes=scratch,
        name=name,
    )(*args)


def from_after(array, axis, shift):
    count = lax.axis_size(axis)
    return lax.ppermute(array, axis, [(i, (i - shift) % count) for i in range(count)])


def local(anomalies, obs_cells, obs_counts, obs_precision, inflation):
    nwin, _, cell_width, members = anomalies.shape
    square = (members, members)
    sent = pick_call(lax.axis_size("cell"), anomalies, obs_cells, obs_counts, obs_precision)
    gathered = lax.all_to_all(sent, "cell", split_axis=0, concat_axis=0, tiled=True)
    part, own = factor_call(gathered, inflation * math.sqrt(members - 1.0))
    other = from_after(own, "tm_2", 1)
    both = simple_call(pair_kernel, "pair", jax.ShapeDtypeStruct(square, BF16), [], own, other)
    pieces = [both] + [from_after(both, "tm_1", s) for s in (1, 2, 3)]
    total, later = simple_call(
        ring_kernel,
        "ring",
        [jax.ShapeDtypeStruct(square, BF16), jax.ShapeDtypeStruct(square, F32)],
        [pltpu.VMEM((4, *square), BF16)],
        *pieces,
    )
    after = [from_after(total, "tm_0", s) for s in (1, 2, 3)]
    inner = simple_call(
        inner_kernel,
        "inner",
        jax.ShapeDtypeStruct((nwin, *square), F32),
        [pltpu.VMEM(square, F32)],
        later,
        other,
        part,
    )
    flat = anomalies.reshape(nwin, 2 * cell_width, members)
    return apply_call(after, inner, flat).reshape(anomalies.shape)


def solution(mesh):
    torus = Mesh(
        mesh.devices.reshape(4, 4, 2, mesh.shape["cell"]), ("tm_0", "tm_1", "tm_2", "cell")
    )
    return jax.shard_map(
        local,
        mesh=torus,
        in_specs=(P(TM, None, "cell", None), P(TM, "cell"), P(TM, "cell"), P(TM, "cell"), P(TM)),
        out_specs=P(TM, None, "cell", None),
        check_vma=False,
    )
```

time: 256 us -> 88.4 us (0.35)
  other arithmetic: 164 us -> 0.51 us
  Pallas kernels: 0 us -> 39.7 us
  blocking collectives: 28.2 us -> 0 us
  matrix products: 14.3 us -> 0 us
  local copies, waits for them, and re-layouts: 18 us -> 4.69 us
  waiting for transfers between devices: 14.9 us -> 25.6 us
  starting transfers between devices: 14 us -> 17.2 us
    another operation x14 -> x0, other arithmetic: 159 us -> none  [the longest x10 100 us: transform_of(): factor = jnp.linalg.cholesky((members - 1.0) * unit_matrix[None] + gram)]
    pallas_call x0 -> x6, Pallas kernels: none -> 39.7 us  [the longest x1 17 us: factor_call(): pl.pallas_call(factor_kernel, in_specs=[pl.BlockSpec(memory_space=pltpu.V...]
    all_gather x3 -> x0, blocking collectives: 28.2 us -> none  [carried_in(): pieces = lax.all_gather(running.astype(jnp.bfloat16), axis)]
    dot_general x20 -> x0, matrix products: 11.9 us -> none  [the longest x18 6.41 us: matmul_f32(): jnp.dot(left, right, precision=lax.Precision.HIGHEST, preferred_element_t...]
    ppermute x0 -> x7, waiting for transfers between devices: none -> 10.8 us  [from_after(): lax.ppermute(array, axis, [(i, (i - shift) % count) for i in range(count)])]
    ppermute x0 -> x7, starting transfers between devices: none -> 8.71 us  [from_after(): lax.ppermute(array, axis, [(i, (i - shift) % count) for i in range(count)])]
    reshape x1 -> x0, local copies, waits for them, and re-layouts: 8.6 us -> none  [local(): return result.astype(jnp.bfloat16).reshape(anomalies.shape)]
    all_to_all x2 -> x1, starting transfers between devices: 14 us -> 8.48 us  [local(): lax.all_to_all(sent, 'cell', split_axis=0, concat_axis=0, tiled=True)]
  transfers between devices with their start and end apart: 2 -> 8, of which waited for: 2 -> 7; matrix products, arithmetic and copies ran while one was open for 3% -> 1% of each run, Pallas kernels for 0% -> 3%
where the time goes in v1:
time: 88.4 us; the launch traced here: 87.8 us
  Pallas kernels  39.7 us (45%)
  waiting for transfers between devices  25.6 us (29%)
  starting transfers between devices  17.2 us (19%)
  local copies, waits for them, and re-layouts  4.69 us (5%)
    pallas_call x1, Pallas kernels, factor_call(): pl.pallas_call(factor_kernel, in_specs=[pl.BlockSpec(memory_space=pltpu.V...  17 us
    all_to_all x1, waiting for transfers between devices, local(): lax.all_to_all(sent, 'cell', split_axis=0, concat_axis=0, tiled=True)  14.9 us
    pallas_call x1, Pallas kernels, apply_call(): pl.pallas_call(apply_kernel, grid=(nwin, rows // step), in_specs=[WHOLE]...  11.7 us
    ppermute x7, waiting for transfers between devices, from_after(): lax.ppermute(array, axis, [(i, (i - shift) % count) for i in range(count)])  10.8 us
    ppermute x7, starting transfers between devices, from_after(): lax.ppermute(array, axis, [(i, (i - shift) % count) for i in range(count)])  8.71 us
    all_to_all x1, starting transfers between devices, local(): lax.all_to_all(sent, 'cell', split_axis=0, concat_axis=0, tiled=True)  8.48 us
    pallas_call x3, Pallas kernels, simple_call(): pl.pallas_call(kernel, in_specs=[WHOLE] * len(args), out_specs=jax.tree.m...  7.54 us
    unnamed x19, local copies, waits for them, and re-layouts  4.69 us
  transfers between devices with their start and end apart: 8, of which 7 were waited for; matrix products, arithmetic and copies ran while one was open for 1% of the time, Pallas kernels for 3%

profile of v1, /device:TPU:6, one launch (start us, length us, event | category | flops | bytes accessed | tf_op | source)
XLA Modules:
  0.0 87.8 jit_solution(6001560251728381170)
XLA Ops:
  0.0 0.0 copy-start.8
  0.0 1.3 %copy.6.counts_ref = s32[3,1]{1,0:T(4,128)} copy(s32[3,1]{0,1:T(1,128)} %param.7) | data formatting | bytes 24 | tf_op args[2]
  1.3 3.4 %pick.1 = bf16[8,104,256]{2,1,0:T(8,128)(2,1)} custom-call(s32[3,32]{1,0:T(4,128)} %cells_ref.1, s32[3,1]{1,0:T(4,128)} %copy.6.counts_ref, f32[3,32]{1,0:T(4,128)} %precision_ref.1, bf16[3,2,2048,256]{3,2,1,0:T(8,128)(2,1)} %field_ref.1), custom_call_target="tpu_custom_call" | custom-call | tf_op jit(solution)/shard_map/pick/pallas_call | solution.py:232
  4.8 8.5 %all-to-all-start = ((bf16[8,104,256]{2,1,0:T(8,128)(2,1)}), bf16[8,104,256]{2,1,0:T(8,128)(2,1)S(1)}, u32[]{:S(2)}, u32[]{:S(2)}) async-start(bf16[8,104,256]{2,1,0:T(8,128)(2,1)} %pick.1), calls=%async_computation | async-start | bytes 851968 | tf_op jit(solution)/shard_map/all_to_all | solution.py:362
  13.2 0.0 copy-done.8
  13.3 0.5 broadcast_multiply_fusion.scale_ref
  13.8 14.9 %all-to-all-done.g_ref = bf16[8,104,256]{2,1,0:T(8,128)(2,1)S(1)} async-done(((bf16[8,104,256]{2,1,0:T(8,128)(2,1)}), bf16[8,104,256]{2,1,0:T(8,128)(2,1)S(1)}, u32[]{:S(2)}, u32[]{:S(2)}) %all-to-all-start) | async-done | bytes 426016 | tf_op jit(solution)/shard_map/all_to_all | solution.py:362
  28.6 0.0 copy-start
  28.7 0.8 copy-done
  29.4 17.0 %factor.1 = (f32[3,256,256]{2,1,0:T(8,128)}, bf16[256,256]{1,0:T(8,128)(2,1)}) custom-call(bf16[8,104,256]{2,1,0:T(8,128)(2,1)} %copy-done, f32[3]{0:T(128)} %broadcast_multiply_fusion.scale_ref), custom_call_target="tpu_custom_call" | custom-call | tf_op jit(solution)/shard_map/factor/pallas_call | solution.py:179
  46.4 0.0 collective-permute-start
  46.4 1.6 %collective-permute-done.other_ref = bf16[256,256]{1,0:T(8,128)(2,1)S(1)} collective-permute-done((bf16[256,256]{1,0:T(8,128)(2,1)}, bf16[256,256]{1,0:T(8,128)(2,1)S(1)}, u32[]{:S(2)}, u32[]{:S(2)}) %collective-permute-start) | collective-permute-done | bytes 131104 | tf_op jit(solution)/shard_map/ppermute | solution.py:355
  48.0 0.0 copy-start.1
  48.0 0.7 copy-done.1
  48.6 1.8 %pair.1.p0 = bf16[256,256]{1,0:T(8,128)(2,1)} custom-call(bf16[256,256]{1,0:T(8,128)(2,1)} %get-tuple-element.9.mine_ref, bf16[256,256]{1,0:T(8,128)(2,1)} %copy-done.1), custom_call_target="tpu_custom_call" | custom-call | tf_op jit(solution)/shard_map/pair/pallas_call | solution.py:343
  50.5 1.6 %collective-permute-start.3 = (bf16[256,256]{1,0:T(8,128)(2,1)}, bf16[256,256]{1,0:T(8,128)(2,1)S(1)}, u32[]{:S(2)}, u32[]{:S(2)}) collective-permute-start(bf16[256,256]{1,0:T(8,128)(2,1)} %pair.1.p0), channel_id=1, source_target_pairs={{0,16},{16,32},{32,48},{48,0},{1,17},{17,33},{33,49},{49,1},{2,18}... | collective-permute-start | bytes 393224 | tf_op jit(solution)/shard_map/ppermute | solution.py:355
  52.0 2.9 %collective-permute-start.2 = (bf16[256,256]{1,0:T(8,128)(2,1)}, bf16[256,256]{1,0:T(8,128)(2,1)S(1)}, u32[]{:S(2)}, u32[]{:S(2)}) collective-permute-start(bf16[256,256]{1,0:T(8,128)(2,1)} %pair.1.p0), channel_id=1, source_target_pairs={{0,32},{16,48},{32,0},{48,16},{1,33},{17,49},{33,1},{49,17},{2,34}... | collective-permute-start | bytes 393224 | tf_op jit(solution)/shard_map/ppermute | solution.py:355
  54.9 1.3 %collective-permute-start.1 = (bf16[256,256]{1,0:T(8,128)(2,1)}, bf16[256,256]{1,0:T(8,128)(2,1)S(1)}, u32[]{:S(2)}, u32[]{:S(2)}) collective-permute-start(bf16[256,256]{1,0:T(8,128)(2,1)} %pair.1.p0), channel_id=1, source_target_pairs={{0,48},{16,0},{32,16},{48,32},{1,49},{17,1},{33,17},{49,33},{2,50}... | collective-permute-start | bytes 393224 | tf_op jit(solution)/shard_map/ppermute | solution.py:355
  56.3 1.2 %collective-permute-done.3.p3 = bf16[256,256]{1,0:T(8,128)(2,1)S(1)} collective-permute-done((bf16[256,256]{1,0:T(8,128)(2,1)}, bf16[256,256]{1,0:T(8,128)(2,1)S(1)}, u32[]{:S(2)}, u32[]{:S(2)}) %collective-permute-start.3) | collective-permute-done | bytes 131104 | tf_op jit(solution)/shard_map/ppermute | solution.py:355
  57.5 0.0 copy-start.5
  57.5 4.0 %collective-permute-done.2.p2 = bf16[256,256]{1,0:T(8,128)(2,1)S(1)} collective-permute-done((bf16[256,256]{1,0:T(8,128)(2,1)}, bf16[256,256]{1,0:T(8,128)(2,1)S(1)}, u32[]{:S(2)}, u32[]{:S(2)}) %collective-permute-start.2) | collective-permute-done | bytes 131104 | tf_op jit(solution)/shard_map/ppermute | solution.py:355
  61.5 0.0 copy-start.6
  61.5 0.0 collective-permute-done.1.p1
  61.5 0.0 copy-done.5
  61.5 0.6 copy-done.6
  62.1 0.0 copy-start.7
  62.1 0.6 copy-done.7
  62.8 2.8 %ring.1 = (bf16[256,256]{1,0:T(8,128)(2,1)}, f32[256,256]{1,0:T(8,128)}) custom-call(bf16[256,256]{1,0:T(8,128)(2,1)} %pair.1.p0, bf16[256,256]{1,0:T(8,128)(2,1)} %copy-done.7, bf16[256,256]{1,0:T(8,128)(2,1)} %copy-done.6, bf16[256,256]{1,0:T(8,128)(2,1)} %copy-done.5), custom_call_target="tpu_custom_call" | custom-call | tf_op jit(solution)/shard_map/ring/pallas_call | solution.py:343
  65.5 0.5 collective-permute-start.6
  66.0 2.4 %collective-permute-start.5 = (bf16[256,256]{1,0:T(8,128)(2,1)}, bf16[256,256]{1,0:T(8,128)(2,1)S(1)}, u32[]{:S(2)}, u32[]{:S(2)}) collective-permute-start(bf16[256,256]{1,0:T(8,128)(2,1)} %get-tuple-element.10), channel_id=1, source_target_pairs={{0,128},{64,192},{128,0},{192,64},{1,129},{65,193},{129,1},{193,65... | collective-permute-start | bytes 393224 | tf_op jit(solution)/shard_map/ppermute | solution.py:355
  68.4 0.0 collective-permute-start.4
  68.4 3.0 %inner.1.inner_ref = f32[3,256,256]{2,1,0:T(8,128)} custom-call(f32[256,256]{1,0:T(8,128)} %get-tuple-element.11.later_ref, bf16[256,256]{1,0:T(8,128)(2,1)} %copy-done.1, f32[3,256,256]{2,1,0:T(8,128)} %get-tuple-element.12.part_ref), custom_call_target="tpu_custom_call" | custom-call | tf_op jit(solution)/shard_map/inner/pallas_call | solution.py:343
  71.4 0.5 collective-permute-done.6.p3
  71.8 0.0 copy-start.2
  71.8 2.3 %collective-permute-done.5.p2 = bf16[256,256]{1,0:T(8,128)(2,1)S(1)} collective-permute-done((bf16[256,256]{1,0:T(8,128)(2,1)}, bf16[256,256]{1,0:T(8,128)(2,1)S(1)}, u32[]{:S(2)}, u32[]{:S(2)}) %collective-permute-start.5) | collective-permute-done | bytes 131104 | tf_op jit(solution)/shard_map/ppermute | solution.py:355
  74.1 0.0 copy-start.3
  74.1 1.3 %collective-permute-done.4.p1 = bf16[256,256]{1,0:T(8,128)(2,1)S(1)} collective-permute-done((bf16[256,256]{1,0:T(8,128)(2,1)}, bf16[256,256]{1,0:T(8,128)(2,1)S(1)}, u32[]{:S(2)}, u32[]{:S(2)}) %collective-permute-start.4) | collective-permute-done | bytes 131104 | tf_op jit(solution)/shard_map/ppermute | solution.py:355
  75.4 0.0 copy-start.4
  75.4 0.0 copy-done.2
  75.4 0.0 copy-done.3
  75.4 0.6 copy-done.4
  76.0 11.7 %apply.1 = bf16[3,4096,256]{2,1,0:T(8,128)(2,1)} custom-call(bf16[256,256]{1,0:T(8,128)(2,1)} %copy-done.4, bf16[256,256]{1,0:T(8,128)(2,1)} %copy-done.3, bf16[256,256]{1,0:T(8,128)(2,1)} %copy-done.2, f32[3,256,256]{2,1,0:T(8,128)} %inner.1.inner_ref, bf16[3,4096,256]{2,1,0:T(8,128)(2,1)} %bitcast.2), custom_call_target="tpu_custom_call" | custom-call | tf_op jit(solution)/shard_map/apply/pallas_call | solution.py:327
Async XLA Ops:
  0.0 13.2 %copy-start.8 = (f32[3]{0:T(128)S(1)}, f32[3]{0:T(128)}, u32[]{:S(2)}) copy-start(f32[3]{0:T(128)} %param.9) | copy-start | bytes 40
  4.8 23.9 %all-to-all-start = ((bf16[8,104,256]{2,1,0:T(8,128)(2,1)}), bf16[8,104,256]{2,1,0:T(8,128)(2,1)S(1)}, u32[]{:S(2)}, u32[]{:S(2)}) async-start(bf16[8,104,256]{2,1,0:T(8,128)(2,1)} %pick.1), calls=%async_computation | async-start | bytes 851968 | tf_op jit(solution)/shard_map/all_to_all | solution.py:362
  28.6 0.8 copy-start
  46.4 1.6 %collective-permute-start = (bf16[256,256]{1,0:T(8,128)(2,1)}, bf16[256,256]{1,0:T(8,128)(2,1)S(1)}, u32[]{:S(2)}, u32[]{:S(2)}) collective-permute-start(bf16[256,256]{1,0:T(8,128)(2,1)} %get-tuple-element.9.mine_ref), channel_id=1, source_target_pairs={{0,8},{8,0},{1,9},{9,1},{2,10},{10,2},{3,11},{11,3},{4,12},{12,4},... | collective-permute-start | bytes 393224 | tf_op jit(solution)/shard_map/ppermute | solution.py:355
  48.0 0.7 copy-start.1
  50.5 7.0 %collective-permute-start.3 = (bf16[256,256]{1,0:T(8,128)(2,1)}, bf16[256,256]{1,0:T(8,128)(2,1)S(1)}, u32[]{:S(2)}, u32[]{:S(2)}) collective-permute-start(bf16[256,256]{1,0:T(8,128)(2,1)} %pair.1.p0), channel_id=1, source_target_pairs={{0,16},{16,32},{32,48},{48,0},{1,17},{17,33},{33,49},{49,1},{2,18}... | collective-permute-start | bytes 393224 | tf_op jit(solution)/shard_map/ppermute | solution.py:355
  52.0 9.4 %collective-permute-start.2 = (bf16[256,256]{1,0:T(8,128)(2,1)}, bf16[256,256]{1,0:T(8,128)(2,1)S(1)}, u32[]{:S(2)}, u32[]{:S(2)}) collective-permute-start(bf16[256,256]{1,0:T(8,128)(2,1)} %pair.1.p0), channel_id=1, source_target_pairs={{0,32},{16,48},{32,0},{48,16},{1,33},{17,49},{33,1},{49,17},{2,34}... | collective-permute-start | bytes 393224 | tf_op jit(solution)/shard_map/ppermute | solution.py:355
  54.9 6.5 %collective-permute-start.1 = (bf16[256,256]{1,0:T(8,128)(2,1)}, bf16[256,256]{1,0:T(8,128)(2,1)S(1)}, u32[]{:S(2)}, u32[]{:S(2)}) collective-permute-start(bf16[256,256]{1,0:T(8,128)(2,1)} %pair.1.p0), channel_id=1, source_target_pairs={{0,48},{16,0},{32,16},{48,32},{1,49},{17,1},{33,17},{49,33},{2,50}... | collective-permute-start | bytes 393224 | tf_op jit(solution)/shard_map/ppermute | solution.py:355
  57.5 4.0 %copy-start.5 = (bf16[256,256]{1,0:T(8,128)(2,1)}, bf16[256,256]{1,0:T(8,128)(2,1)S(1)}, u32[]{:S(2)}) copy-start(bf16[256,256]{1,0:T(8,128)(2,1)S(1)} %collective-permute-done.3.p3) | copy-start | bytes 393220
  61.5 0.6 copy-start.6
  62.1 0.6 copy-start.7
  65.5 6.3 %collective-permute-start.6 = (bf16[256,256]{1,0:T(8,128)(2,1)}, bf16[256,256]{1,0:T(8,128)(2,1)S(1)}, u32[]{:S(2)}, u32[]{:S(2)}) collective-permute-start(bf16[256,256]{1,0:T(8,128)(2,1)} %get-tuple-element.10), channel_id=1, source_target_pairs={{0,64},{64,128},{128,192},{192,0},{1,65},{65,129},{129,193},{193,1... | collective-permute-start | bytes 393224 | tf_op jit(solution)/shard_map/ppermute | solution.py:355
  66.0 8.1 %collective-permute-start.5 = (bf16[256,256]{1,0:T(8,128)(2,1)}, bf16[256,256]{1,0:T(8,128)(2,1)S(1)}, u32[]{:S(2)}, u32[]{:S(2)}) collective-permute-start(bf16[256,256]{1,0:T(8,128)(2,1)} %get-tuple-element.10), channel_id=1, source_target_pairs={{0,128},{64,192},{128,0},{192,64},{1,129},{65,193},{129,1},{193,65... | collective-permute-start | bytes 393224 | tf_op jit(solution)/shard_map/ppermute | solution.py:355
  68.4 7.0 %collective-permute-start.4 = (bf16[256,256]{1,0:T(8,128)(2,1)}, bf16[256,256]{1,0:T(8,128)(2,1)S(1)}, u32[]{:S(2)}, u32[]{:S(2)}) collective-permute-start(bf16[256,256]{1,0:T(8,128)(2,1)} %get-tuple-element.10), channel_id=1, source_target_pairs={{0,192},{64,0},{128,64},{192,128},{1,193},{65,1},{129,65},{193,129... | collective-permute-start | bytes 393224 | tf_op jit(solution)/shard_map/ppermute | solution.py:355
  71.8 3.6 %copy-start.2 = (bf16[256,256]{1,0:T(8,128)(2,1)}, bf16[256,256]{1,0:T(8,128)(2,1)S(1)}, u32[]{:S(2)}) copy-start(bf16[256,256]{1,0:T(8,128)(2,1)S(1)} %collective-permute-done.6.p3) | copy-start | bytes 393220
  74.1 1.3 %copy-start.3 = (bf16[256,256]{1,0:T(8,128)(2,1)}, bf16[256,256]{1,0:T(8,128)(2,1)S(1)}, u32[]{:S(2)}) copy-start(bf16[256,256]{1,0:T(8,128)(2,1)S(1)} %collective-permute-done.5.p2) | copy-start | bytes 393220
  75.4 0.7 copy-start.4

commit v2 on v1

--- a/solution.py
+++ b/solution.py
@@ -9,7 +9,8 @@
 from jax.sharding import PartitionSpec as P
 
 TM = ("tm_0", "tm_1", "tm_2")
-VMEM = pltpu.VMEM
+WHOLE = pl.BlockSpec(memory_space=pltpu.VMEM)
+SCALARS = pl.BlockSpec(memory_space=pltpu.SMEM)
 F32 = jnp.float32
 BF16 = jnp.bfloat16
 HI = lax.Precision.HIGHEST
@@ -129,20 +130,23 @@
             zero = jnp.zeros((B, 128), F32)
             wide = jnp.concatenate([moved, zero] if half == 0 else [zero, moved], axis=1)
             qw = jnp.where(inside, wide, q[w * B : (w + 1) * B])
-            qs.append((qw, moved))
+            qs.append(qw)
             X[k, w * B : (w + 1) * B, :] = jnp.where(lane_q < (k + 1) * B, qw, 0.0)
+        if k + 1 == nb:
+            continue
         for w in range(nwin):
-            qw, moved = qs[w]
-            if k + 1 == nb:
-                continue
+            q1, q2, q3 = split3(qs[w])
+            start = 128 * ((k + 1) * B // 128)
+            left = jnp.concatenate([q1, q1, q1, q2, q2, q3], axis=0)[:, start:].T
+            right = jnp.concatenate([q1, q2, q3, q1, q2, q1], axis=0)
+            upd = dot(left[(k + 1) * B - start :], right).reshape(nb - k - 1, B, 256)
             below = X[k + 1 :, w * B : (w + 1) * B, :]
-            nrow = (nb - k - 1) * B
-            p = dot_nt(below[:, :, half * 128 : half * 128 + 128].reshape(nrow, 128), moved, HI)
-            upd = dot(p, qw, HI).reshape(nb - k - 1, B, 256)
             X[k + 1 :, w * B : (w + 1) * B, :] = jnp.where(inside[None], 0.0, below) - upd
 
 
-def factor_kernel(g_ref, scale_ref, part_ref, own_ref, X, Y):
+def factor_kernel(g_ref, scale_ref, far_ref, part_ref, own_ref, near_ref, X, Y, sem):
+    fetch = pltpu.make_async_copy(far_ref, near_ref, sem)
+    fetch.start()
     nz = g_ref.shape[0]
     nwin = scale_ref.shape[0]
     slots = 32
@@ -171,23 +175,29 @@
         x = X[:, w * B : (w + 1) * B, :].reshape(256, 256) * scale_ref[w]
         s = x if s is None else dot_x3(s, x)
         part_ref[w] = s
-    own_ref[...] = s.astype(BF16)
-
-
-def factor_call(g, scale):
+    own_ref[...] = pack(s).astype(BF16)
+    fetch.wait()
+
+
+def factor_call(g, scale, flat):
     nwin = scale.shape[0]
     return pl.pallas_call(
         factor_kernel,
-        in_specs=[pl.BlockSpec(memory_space=pltpu.VMEM), pl.BlockSpec(memory_space=pltpu.SMEM)],
-        out_specs=[pl.BlockSpec(memory_space=pltpu.VMEM)] * 2,
-        out_shape=[jax.ShapeDtypeStruct((nwin, 256, 256), F32), jax.ShapeDtypeStruct((256, 256), BF16)],
-        scratch_shapes=[pltpu.VMEM((256 // B, nwin * B, 256), F32), pltpu.VMEM((nwin, 256, 256), BF16)],
+        in_specs=[WHOLE, SCALARS, pl.BlockSpec(memory_space=pltpu.HBM)],
+        out_specs=[WHOLE] * 3,
+        out_shape=[
+            jax.ShapeDtypeStruct((nwin, 256, 256), F32),
+            PACKED,
+            pltpu.VMEM(flat.shape, BF16),
+        ],
+        scratch_shapes=[
+            pltpu.VMEM((256 // B, nwin * B, 256), F32),
+            pltpu.VMEM((nwin, 256, 256), BF16),
+            pltpu.SemaphoreType.DMA,
+        ],
+        compiler_params=pltpu.CompilerParams(vmem_limit_bytes=12 << 20),
         name="factor",
-    )(g, scale)
-
-
-WHOLE = pl.BlockSpec(memory_space=pltpu.VMEM)
-SCALARS = pl.BlockSpec(memory_space=pltpu.SMEM)
+    )(g, scale, pltpu.with_memory_space_constraint(flat, pltpu.HBM))
 
 
 def pick_kernel(cells_ref, counts_ref, precision_ref, field_ref, out_ref, near, row_scr, sem):
@@ -205,7 +215,7 @@
     row_scr[...] = jnp.zeros(row_scr.shape, F32)
     lane = lax.broadcasted_iota(jnp.int32, (1, slots), 1)
     for w in range(nwin):
-        row_scr[w : w + 1, :slots] = jnp.where(lane < counts_ref[w, 0], precision_ref[w : w + 1, :], 0.0)
+        row_scr[w : w + 1, :slots] = jnp.where(lane < counts_ref[w], precision_ref[w : w + 1, :], 0.0)
     live = row_scr[...]
     high = live.astype(BF16)
     low = (live - high.astype(F32)).astype(BF16)
@@ -231,7 +241,7 @@
     members = anomalies.shape[3]
     return pl.pallas_call(
         pick_kernel,
-        in_specs=[SCALARS, SCALARS, WHOLE, pl.BlockSpec(memory_space=pl.ANY)],
+        in_specs=[SCALARS, SCALARS, WHOLE, pl.BlockSpec(memory_space=pltpu.HBM)],
         out_specs=WHOLE,
         out_shape=jax.ShapeDtypeStruct((copies, nwin * slots + 8, members), BF16),
         scratch_shapes=[
@@ -240,30 +250,46 @@
             pltpu.SemaphoreType.DMA,
         ],
         name="pick",
-    )(obs_cells, obs_counts, obs_precision, anomalies)
+    )(obs_cells, obs_counts, obs_precision, pltpu.with_memory_space_constraint(anomalies, pltpu.HBM))
 
 
 def identity_bf16(n):
     return (lax.broadcasted_iota(jnp.int32, (n, n), 0) == lax.broadcasted_iota(jnp.int32, (n, n), 1)).astype(BF16)
 
 
+def pack(s):
+    h = 64
+    top = jnp.concatenate([s[:h, :128][:, :h], s[128 : 128 + h, 128:][:, :h]], axis=1)
+    return jnp.concatenate([top, s[h:128, :128], s[128 + h :, 128:], s[128:, :128]], axis=0)
+
+
+def unpack(p):
+    h = 64
+    zero = jnp.zeros((h, h), p.dtype)
+    first = jnp.concatenate([jnp.concatenate([p[:h, :h], zero], axis=1), p[h : 2 * h]], axis=0)
+    last = jnp.concatenate([jnp.concatenate([p[:h, h:], zero], axis=1), p[2 * h : 3 * h]], axis=0)
+    upper = jnp.concatenate([first, jnp.zeros((128, 128), p.dtype)], axis=1)
+    lower = jnp.concatenate([p[3 * h :], last], axis=1)
+    return jnp.concatenate([upper, lower], axis=0)
+
+
+PACKED = jax.ShapeDtypeStruct((320, 128), jnp.bfloat16)
+
+
 def pair_kernel(mine_ref, other_ref, both_ref):
     core = lax.axis_index("tm_2")
-    first = jnp.where(core == 0, mine_ref[...].astype(F32), other_ref[...].astype(F32)).astype(BF16)
-    second = jnp.where(core == 0, other_ref[...].astype(F32), mine_ref[...].astype(F32)).astype(BF16)
-    both_ref[...] = dot(second, first).astype(BF16)
-
-
-def later_of(q, me):
-    return [lambda: dot_x3(dot(q[3], q[2]), q[1].astype(F32)), lambda: dot(q[3], q[2]), lambda: q[3].astype(F32)]
+    mine, other = mine_ref[...].astype(F32), other_ref[...].astype(F32)
+    first = unpack(jnp.where(core == 0, mine, other)).astype(BF16)
+    second = unpack(jnp.where(core == 0, other, mine)).astype(BF16)
+    both_ref[...] = pack(dot(second, first)).astype(BF16)
 
 
 def ring_kernel(p0, p1, p2, p3, total_ref, later_ref, q):
     me = lax.axis_index("tm_1")
     for s, piece in enumerate((p0, p1, p2, p3)):
-        q[lax.rem(me + s, 4)] = piece[...]
+        q[lax.rem(me + s, 4)] = unpack(piece[...].astype(F32)).astype(BF16)
     high = dot(q[3], q[2])
-    total_ref[...] = dot_x3(high, dot(q[1], q[0])).astype(BF16)
+    total_ref[...] = pack(dot_x3(high, dot(q[1], q[0]))).astype(BF16)
     later_ref[...] = high
 
     @pl.when(me == 0)
@@ -285,56 +311,64 @@
 
     @pl.when(core == 0)
     def _():
-        before[...] = dot_x3(later_ref[...], other_ref[...].astype(F32))
+        before[...] = dot_x3(later_ref[...], unpack(other_ref[...].astype(F32)))
 
     for w in range(part_ref.shape[0]):
         out_ref[w] = dot_x3(before[...], part_ref[w])
 
 
-def apply_kernel(p1, p2, p3, inner_ref, field_ref, out_ref, q, later, weights):
-    @pl.when((pl.program_id(0) == 0) & (pl.program_id(1) == 0))
-    def _():
-        me = lax.axis_index("tm_0")
-        for s, piece in enumerate((p1, p2, p3)):
-            q[lax.rem(me + s + 1, 4)] = piece[...]
-
-        @pl.when(me == 0)
-        def _():
-            later[...] = dot_x3(dot(q[3], q[2]), q[1].astype(F32))
-
-        @pl.when(me == 1)
-        def _():
-            later[...] = dot(q[3], q[2])
-
-        @pl.when(me == 2)
-        def _():
-            later[...] = q[3].astype(F32)
-
-        @pl.when(me == 3)
-        def _():
-            later[...] = identity_bf16(256).astype(F32)
-
-        for w in range(inner_ref.shape[0]):
-            weights[w] = dot_x3(later[...], inner_ref[w]).astype(BF16)
-
-    out_ref[0] = dot_nt(field_ref[0], weights[pl.program_id(0)]).astype(BF16)
+def apply_kernel(p1, p2, p3, inner_ref, field_ref, out_ref, q, later, result, sems):
+    me = lax.axis_index("tm_0")
+    for s, piece in enumerate((p1, p2, p3)):
+        q[lax.rem(me + s + 1, 4)] = unpack(piece[...].astype(F32)).astype(BF16)
+
+    @pl.when(me == 0)
+    def _():
+        later[...] = dot_x3(dot(q[3], q[2]), q[1].astype(F32))
+
+    @pl.when(me == 1)
+    def _():
+        later[...] = dot(q[3], q[2])
+
+    @pl.when(me == 2)
+    def _():
+        later[...] = q[3].astype(F32)
+
+    @pl.when(me == 3)
+    def _():
+        later[...] = identity_bf16(256).astype(F32)
+
+    nwin, rows, _ = field_ref.shape
+    copies = []
+    for w in range(nwin):
+        weights = dot_x3(later[...], inner_ref[w]).T.astype(BF16)
+        for half in range(STEPS):
+            span = pl.ds(half * (rows // STEPS), rows // STEPS)
+            result[w, span, :] = dot(field_ref[w, span, :], weights).astype(BF16)
+            copy = pltpu.make_async_copy(result.at[w, span], out_ref.at[w, span], sems.at[w, half])
+            copy.start()
+            copies.append(copy)
+    for copy in copies:
+        copy.wait()
+
+
+STEPS = 2
 
 
 def apply_call(pieces, inner, flat):
     nwin, rows, members = flat.shape
-    step = 1024
-    block = pl.BlockSpec((1, step, members), lambda w, i: (w, i, 0))
     return pl.pallas_call(
         apply_kernel,
-        grid=(nwin, rows // step),
-        in_specs=[WHOLE] * 4 + [block],
-        out_specs=block,
+        in_specs=[WHOLE] * 5,
+        out_specs=pl.BlockSpec(memory_space=pltpu.HBM),
         out_shape=jax.ShapeDtypeStruct(flat.shape, BF16),
         scratch_shapes=[
             pltpu.VMEM((4, members, members), BF16),
             pltpu.VMEM((members, members), F32),
-            pltpu.VMEM((nwin, members, members), BF16),
+            pltpu.VMEM(flat.shape, BF16),
+            pltpu.SemaphoreType.DMA((nwin, STEPS)),
         ],
+        compiler_params=pltpu.CompilerParams(vmem_limit_bytes=24 << 20),
         name="apply",
     )(*pieces, inner, flat)
 
@@ -346,6 +380,7 @@
         out_specs=jax.tree.map(lambda _: WHOLE, out_shape),
         out_shape=out_shape,
         scratch_shapes=scratch,
+        compiler_params=pltpu.CompilerParams(vmem_limit_bytes=8 << 20),
         name=name,
     )(*args)
 
@@ -358,16 +393,17 @@
 def local(anomalies, obs_cells, obs_counts, obs_precision, inflation):
     nwin, _, cell_width, members = anomalies.shape
     square = (members, members)
-    sent = pick_call(lax.axis_size("cell"), anomalies, obs_cells, obs_counts, obs_precision)
+    sent = pick_call(lax.axis_size("cell"), anomalies, obs_cells, obs_counts.reshape(nwin), obs_precision)
+    flat = anomalies.reshape(nwin, 2 * cell_width, members)
     gathered = lax.all_to_all(sent, "cell", split_axis=0, concat_axis=0, tiled=True)
-    part, own = factor_call(gathered, inflation * math.sqrt(members - 1.0))
+    part, own, near = factor_call(gathered, inflation * math.sqrt(members - 1.0), flat)
     other = from_after(own, "tm_2", 1)
-    both = simple_call(pair_kernel, "pair", jax.ShapeDtypeStruct(square, BF16), [], own, other)
+    both = simple_call(pair_kernel, "pair", PACKED, [], own, other)
     pieces = [both] + [from_after(both, "tm_1", s) for s in (1, 2, 3)]
     total, later = simple_call(
         ring_kernel,
         "ring",
-        [jax.ShapeDtypeStruct(square, BF16), jax.ShapeDtypeStruct(square, F32)],
+        [PACKED, jax.ShapeDtypeStruct(square, F32)],
         [pltpu.VMEM((4, *square), BF16)],
         *pieces,
     )
@@ -381,8 +417,7 @@
         other,
         part,
     )
-    flat = anomalies.reshape(nwin, 2 * cell_width, members)
-    return apply_call(after, inner, flat).reshape(anomalies.shape)
+    return apply_call(after, inner, near).reshape(anomalies.shape)
 
 
 def solution(mesh):

time: 88.4 us -> 68 us (0.77)
  Pallas kernels: 39.7 us -> 25.3 us
  local copies, waits for them, and re-layouts: 4.69 us -> 0.01 us
  waiting for transfers between devices: 25.6 us -> 24.5 us
    pallas_call x2, Pallas kernels: 28.7 us -> 19.6 us  [the longest x1 15 us: factor_call(): pl.pallas_call(factor_kernel, in_specs=[WHOLE, SCALARS, pl.BlockSpec(memo...]
    pallas_call x3, Pallas kernels: 7.54 us -> 2.13 us  [simple_call(): pl.pallas_call(kernel, in_specs=[WHOLE] * len(args), out_specs=jax.tree.m...]
    unnamed x19 -> x2, local copies, waits for them, and re-layouts: 4.69 us -> 0.01 us
    ppermute x7, waiting for transfers between devices: 10.8 us -> 9.16 us  [from_after(): lax.ppermute(array, axis, [(i, (i - shift) % count) for i in range(count)])]
  transfers between devices with their start and end apart: 8 -> 8, of which waited for: 7 -> 7; matrix products, arithmetic and copies ran while one was open for 1% -> 0% of each run, Pallas kernels for 3% -> 1%
where the time goes in v2:
time: 68 us; the launch traced here: 67.7 us
  Pallas kernels  25.3 us (37%)
  waiting for transfers between devices  24.5 us (36%)
  starting transfers between devices  17.6 us (26%)
    all_to_all x1, waiting for transfers between devices, local(): lax.all_to_all(sent, 'cell', split_axis=0, concat_axis=0, tiled=True)  15.4 us
    pallas_call x1, Pallas kernels, factor_call(): pl.pallas_call(factor_kernel, in_specs=[WHOLE, SCALARS, pl.BlockSpec(memo...  15 us
    ppermute x7, waiting for transfers between devices, from_after(): lax.ppermute(array, axis, [(i, (i - shift) % count) for i in range(count)])  9.16 us
    ppermute x7, starting transfers between devices, from_after(): lax.ppermute(array, axis, [(i, (i - shift) % count) for i in range(count)])  9.15 us
    all_to_all x1, starting transfers between devices, local(): lax.all_to_all(sent, 'cell', split_axis=0, concat_axis=0, tiled=True)  8.48 us
    pallas_call x1, Pallas kernels, apply_call(): pl.pallas_call(apply_kernel, in_specs=[WHOLE] * 5, out_specs=pl.BlockSpec...  4.65 us
    pallas_call x1, Pallas kernels, pick_call(): pl.pallas_call(pick_kernel, in_specs=[SCALARS, SCALARS, WHOLE, pl.BlockSp...  3.53 us
    pallas_call x3, Pallas kernels, simple_call(): pl.pallas_call(kernel, in_specs=[WHOLE] * len(args), out_specs=jax.tree.m...  2.13 us
  transfers between devices with their start and end apart: 8, of which 7 were waited for; matrix products, arithmetic and copies ran while one was open for 0% of the time, Pallas kernels for 1%

profile of v2, /device:TPU:6, one launch (start us, length us, event | category | flops | bytes accessed | tf_op | source)
XLA Modules:
  0.0 67.7 jit_solution(3672875453716242026)
XLA Ops:
  0.0 0.0 copy-start
  0.0 3.5 %pick.1 = bf16[8,104,256]{2,1,0:T(8,128)(2,1)} custom-call(s32[3,32]{1,0:T(4,128)} %cells_ref.1, s32[3]{0:T(128)} %bitcast.4, f32[3,32]{1,0:T(4,128)} %precision_ref.1, bf16[3,2,2048,256]{3,2,1,0:T(8,128)(2,1)} %field_ref.1), custom_call_target="tpu_custom_call" | custom-call | tf_op jit(solution)/shard_map/pick/pallas_call | solution.py:242
  3.5 8.5 %all-to-all-start = ((bf16[8,104,256]{2,1,0:T(8,128)(2,1)}), bf16[8,104,256]{2,1,0:T(8,128)(2,1)S(1)}, u32[]{:S(2)}, u32[]{:S(2)}) async-start(bf16[8,104,256]{2,1,0:T(8,128)(2,1)} %pick.1), calls=%async_computation | async-start | bytes 851968 | tf_op jit(solution)/shard_map/all_to_all | solution.py:398
  12.0 0.0 copy-done
  12.0 15.4 %all-to-all-done.g_ref = bf16[8,104,256]{2,1,0:T(8,128)(2,1)S(1)} async-done(((bf16[8,104,256]{2,1,0:T(8,128)(2,1)}), bf16[8,104,256]{2,1,0:T(8,128)(2,1)S(1)}, u32[]{:S(2)}, u32[]{:S(2)}) %all-to-all-start) | async-done | bytes 426016 | tf_op jit(solution)/shard_map/all_to_all | solution.py:398
  27.4 15.0 %factor.1 = (f32[3,256,256]{2,1,0:T(8,128)S(1)}, bf16[320,128]{1,0:T(8,128)(2,1)S(1)}, bf16[3,4096,256]{2,1,0:T(8,128)(2,1)S(1)}) custom-call(bf16[8,104,256]{2,1,0:T(8,128)(2,1)S(1)} %all-to-all-done.g_ref, f32[3]{0:T(128)S(1)} %broadcast_multiply_fusion.scale_ref, bf16[3,4096,256]{2,1,0:T(8,128)(2,1)} %bitcast.3), custom_call_target="tpu_custom_call" | custom-call | tf_op jit(solution)/shard_map/factor/pallas_call | solution.py:184
  42.4 0.1 collective-permute-start
  42.5 1.3 %collective-permute-done.other_ref = bf16[320,128]{1,0:T(8,128)(2,1)S(1)} collective-permute-done((bf16[320,128]{1,0:T(8,128)(2,1)S(1)}, bf16[320,128]{1,0:T(8,128)(2,1)S(1)}, u32[]{:S(2)}, u32[]{:S(2)}) %collective-permute-start) | collective-permute-done | bytes 81952 | tf_op jit(solution)/shard_map/ppermute | solution.py:390
  43.8 0.3 pair.1.p0
  44.1 1.6 %collective-permute-start.3 = (bf16[320,128]{1,0:T(8,128)(2,1)S(1)}, bf16[320,128]{1,0:T(8,128)(2,1)S(1)}, u32[]{:S(2)}, u32[]{:S(2)}) collective-permute-start(bf16[320,128]{1,0:T(8,128)(2,1)S(1)} %pair.1.p0), channel_id=1, source_target_pairs={{0,16},{16,32},{32,48},{48,0},{1,17},{17,33},{33,49},{49,1},{2,18}... | collective-permute-start | bytes 245768 | tf_op jit(solution)/shard_map/ppermute | solution.py:390
  45.7 2.9 %collective-permute-start.2 = (bf16[320,128]{1,0:T(8,128)(2,1)S(1)}, bf16[320,128]{1,0:T(8,128)(2,1)S(1)}, u32[]{:S(2)}, u32[]{:S(2)}) collective-permute-start(bf16[320,128]{1,0:T(8,128)(2,1)S(1)} %pair.1.p0), channel_id=1, source_target_pairs={{0,32},{16,48},{32,0},{48,16},{1,33},{17,49},{33,1},{49,17},{2,34}... | collective-permute-start | bytes 245768 | tf_op jit(solution)/shard_map/ppermute | solution.py:390
  48.6 1.3 %collective-permute-start.1 = (bf16[320,128]{1,0:T(8,128)(2,1)S(1)}, bf16[320,128]{1,0:T(8,128)(2,1)S(1)}, u32[]{:S(2)}, u32[]{:S(2)}) collective-permute-start(bf16[320,128]{1,0:T(8,128)(2,1)S(1)} %pair.1.p0), channel_id=1, source_target_pairs={{0,48},{16,0},{32,16},{48,32},{1,49},{17,1},{33,17},{49,33},{2,50}... | collective-permute-start | bytes 245768 | tf_op jit(solution)/shard_map/ppermute | solution.py:390
  50.0 0.0 collective-permute-done.3.p3
  50.0 2.9 %collective-permute-done.2.p2 = bf16[320,128]{1,0:T(8,128)(2,1)S(1)} collective-permute-done((bf16[320,128]{1,0:T(8,128)(2,1)S(1)}, bf16[320,128]{1,0:T(8,128)(2,1)S(1)}, u32[]{:S(2)}, u32[]{:S(2)}) %collective-permute-start.2) | collective-permute-done | bytes 81952 | tf_op jit(solution)/shard_map/ppermute | solution.py:390
  52.9 0.2 collective-permute-done.1.p1
  53.1 1.0 %ring.1 = (bf16[320,128]{1,0:T(8,128)(2,1)S(1)}, f32[256,256]{1,0:T(8,128)S(1)}) custom-call(bf16[320,128]{1,0:T(8,128)(2,1)S(1)} %pair.1.p0, bf16[320,128]{1,0:T(8,128)(2,1)S(1)} %collective-permute-done.1.p1, bf16[320,128]{1,0:T(8,128)(2,1)S(1)} %collective-permute-done.2.p2, bf16[320,128]{1,0:T(8,128)(2,1)S(1)} %collective-permute-done.3.p3), custom_call_target="tpu_custom_call" | custom-call | tf_op jit(solution)/shard_map/ring/pallas_call | solution.py:377
  54.1 0.7 %collective-permute-start.6 = (bf16[320,128]{1,0:T(8,128)(2,1)S(1)}, bf16[320,128]{1,0:T(8,128)(2,1)S(1)}, u32[]{:S(2)}, u32[]{:S(2)}) collective-permute-start(bf16[320,128]{1,0:T(8,128)(2,1)S(1)} %get-tuple-element.11), channel_id=1, source_target_pairs={{0,64},{64,128},{128,192},{192,0},{1,65},{65,129},{129,193},{193,1... | collective-permute-start | bytes 245768 | tf_op jit(solution)/shard_map/ppermute | solution.py:390
  54.8 2.4 %collective-permute-start.5 = (bf16[320,128]{1,0:T(8,128)(2,1)S(1)}, bf16[320,128]{1,0:T(8,128)(2,1)S(1)}, u32[]{:S(2)}, u32[]{:S(2)}) collective-permute-start(bf16[320,128]{1,0:T(8,128)(2,1)S(1)} %get-tuple-element.11), channel_id=1, source_target_pairs={{0,128},{64,192},{128,0},{192,64},{1,129},{65,193},{129,1},{193,65... | collective-permute-start | bytes 245768 | tf_op jit(solution)/shard_map/ppermute | solution.py:390
  57.2 0.0 collective-permute-start.4
  57.2 0.8 %inner.1.inner_ref = f32[3,256,256]{2,1,0:T(8,128)S(1)} custom-call(f32[256,256]{1,0:T(8,128)S(1)} %get-tuple-element.12.later_ref, bf16[320,128]{1,0:T(8,128)(2,1)S(1)} %collective-permute-done.other_ref, f32[3,256,256]{2,1,0:T(8,128)S(1)} %get-tuple-element.13.part_ref), custom_call_target="tpu_custom_call" | custom-call | tf_op jit(solution)/shard_map/inner/pallas_call | solution.py:377
  58.1 0.7 %collective-permute-done.6.p3 = bf16[320,128]{1,0:T(8,128)(2,1)S(1)} collective-permute-done((bf16[320,128]{1,0:T(8,128)(2,1)S(1)}, bf16[320,128]{1,0:T(8,128)(2,1)S(1)}, u32[]{:S(2)}, u32[]{:S(2)}) %collective-permute-start.6) | collective-permute-done | bytes 81952 | tf_op jit(solution)/shard_map/ppermute | solution.py:390
  58.8 2.6 %collective-permute-done.5.p2 = bf16[320,128]{1,0:T(8,128)(2,1)S(1)} collective-permute-done((bf16[320,128]{1,0:T(8,128)(2,1)S(1)}, bf16[320,128]{1,0:T(8,128)(2,1)S(1)}, u32[]{:S(2)}, u32[]{:S(2)}) %collective-permute-start.5) | collective-permute-done | bytes 81952 | tf_op jit(solution)/shard_map/ppermute | solution.py:390
  61.3 1.5 %collective-permute-done.4.p1 = bf16[320,128]{1,0:T(8,128)(2,1)S(1)} collective-permute-done((bf16[320,128]{1,0:T(8,128)(2,1)S(1)}, bf16[320,128]{1,0:T(8,128)(2,1)S(1)}, u32[]{:S(2)}, u32[]{:S(2)}) %collective-permute-start.4) | collective-permute-done | bytes 81952 | tf_op jit(solution)/shard_map/ppermute | solution.py:390
  62.9 4.6 %apply.1 = bf16[3,4096,256]{2,1,0:T(8,128)(2,1)} custom-call(bf16[320,128]{1,0:T(8,128)(2,1)S(1)} %collective-permute-done.4.p1, bf16[320,128]{1,0:T(8,128)(2,1)S(1)} %collective-permute-done.5.p2, bf16[320,128]{1,0:T(8,128)(2,1)S(1)} %collective-permute-done.6.p3, f32[3,256,256]{2,1,0:T(8,128)S(1)} %inner.1.inner_ref, ...), custom_call_target="tpu_custom_call" | custom-call | tf_op jit(solution)/shard_map/apply/pallas_call | solution.py:360
  (1 shorter events, 0.0 us)
Async XLA Ops:
  0.0 12.0 %copy-start = (f32[3]{0:T(128)S(1)}, f32[3]{0:T(128)}, u32[]{:S(2)}) copy-start(f32[3]{0:T(128)} %param.9) | copy-start | bytes 40
  3.5 23.9 %all-to-all-start = ((bf16[8,104,256]{2,1,0:T(8,128)(2,1)}), bf16[8,104,256]{2,1,0:T(8,128)(2,1)S(1)}, u32[]{:S(2)}, u32[]{:S(2)}) async-start(bf16[8,104,256]{2,1,0:T(8,128)(2,1)} %pick.1), calls=%async_computation | async-start | bytes 851968 | tf_op jit(solution)/shard_map/all_to_all | solution.py:398
  42.4 1.4 %collective-permute-start = (bf16[320,128]{1,0:T(8,128)(2,1)S(1)}, bf16[320,128]{1,0:T(8,128)(2,1)S(1)}, u32[]{:S(2)}, u32[]{:S(2)}) collective-permute-start(bf16[320,128]{1,0:T(8,128)(2,1)S(1)} %get-tuple-element.10.mine_ref), channel_id=1, source_target_pairs={{0,8},{8,0},{1,9},{9,1},{2,10},{10,2},{3,11},{11,3},{4,12},{12,4},... | collective-permute-start | bytes 245768 | tf_op jit(solution)/shard_map/ppermute | solution.py:390
  44.1 5.9 %collective-permute-start.3 = (bf16[320,128]{1,0:T(8,128)(2,1)S(1)}, bf16[320,128]{1,0:T(8,128)(2,1)S(1)}, u32[]{:S(2)}, u32[]{:S(2)}) collective-permute-start(bf16[320,128]{1,0:T(8,128)(2,1)S(1)} %pair.1.p0), channel_id=1, source_target_pairs={{0,16},{16,32},{32,48},{48,0},{1,17},{17,33},{33,49},{49,1},{2,18}... | collective-permute-start | bytes 245768 | tf_op jit(solution)/shard_map/ppermute | solution.py:390
  45.7 7.1 %collective-permute-start.2 = (bf16[320,128]{1,0:T(8,128)(2,1)S(1)}, bf16[320,128]{1,0:T(8,128)(2,1)S(1)}, u32[]{:S(2)}, u32[]{:S(2)}) collective-permute-start(bf16[320,128]{1,0:T(8,128)(2,1)S(1)} %pair.1.p0), channel_id=1, source_target_pairs={{0,32},{16,48},{32,0},{48,16},{1,33},{17,49},{33,1},{49,17},{2,34}... | collective-permute-start | bytes 245768 | tf_op jit(solution)/shard_map/ppermute | solution.py:390
  48.6 4.4 %collective-permute-start.1 = (bf16[320,128]{1,0:T(8,128)(2,1)S(1)}, bf16[320,128]{1,0:T(8,128)(2,1)S(1)}, u32[]{:S(2)}, u32[]{:S(2)}) collective-permute-start(bf16[320,128]{1,0:T(8,128)(2,1)S(1)} %pair.1.p0), channel_id=1, source_target_pairs={{0,48},{16,0},{32,16},{48,32},{1,49},{17,1},{33,17},{49,33},{2,50}... | collective-permute-start | bytes 245768 | tf_op jit(solution)/shard_map/ppermute | solution.py:390
  54.1 4.7 %collective-permute-start.6 = (bf16[320,128]{1,0:T(8,128)(2,1)S(1)}, bf16[320,128]{1,0:T(8,128)(2,1)S(1)}, u32[]{:S(2)}, u32[]{:S(2)}) collective-permute-start(bf16[320,128]{1,0:T(8,128)(2,1)S(1)} %get-tuple-element.11), channel_id=1, source_target_pairs={{0,64},{64,128},{128,192},{192,0},{1,65},{65,129},{129,193},{193,1... | collective-permute-start | bytes 245768 | tf_op jit(solution)/shard_map/ppermute | solution.py:390
  54.8 6.5 %collective-permute-start.5 = (bf16[320,128]{1,0:T(8,128)(2,1)S(1)}, bf16[320,128]{1,0:T(8,128)(2,1)S(1)}, u32[]{:S(2)}, u32[]{:S(2)}) collective-permute-start(bf16[320,128]{1,0:T(8,128)(2,1)S(1)} %get-tuple-element.11), channel_id=1, source_target_pairs={{0,128},{64,192},{128,0},{192,64},{1,129},{65,193},{129,1},{193,65... | collective-permute-start | bytes 245768 | tf_op jit(solution)/shard_map/ppermute | solution.py:390
  57.2 5.7 %collective-permute-start.4 = (bf16[320,128]{1,0:T(8,128)(2,1)S(1)}, bf16[320,128]{1,0:T(8,128)(2,1)S(1)}, u32[]{:S(2)}, u32[]{:S(2)}) collective-permute-start(bf16[320,128]{1,0:T(8,128)(2,1)S(1)} %get-tuple-element.11), channel_id=1, source_target_pairs={{0,192},{64,0},{128,64},{192,128},{1,193},{65,1},{129,65},{193,129... | collective-permute-start | bytes 245768 | tf_op jit(solution)/shard_map/ppermute | solution.py:390

commit v3 on v2

--- a/solution.py
+++ b/solution.py
@@ -57,30 +57,42 @@
     local = lane - base
     roots = []
     for t in range(n):
-        cols = []
-        for i in range(T):
-            index = base + (t * T + i)
-            cols.append([jnp.take_along_axis(tiles[r], index, axis=1) if r >= t else None for r in range(n)])
+        cols = [[None] * n for _ in range(T)]
+        for r in range(t, n):
+            index = base + r * T + sub
+            for i in range(T):
+                cols[i][r] = jnp.take_along_axis(row_of(tiles[t], i), index, axis=1)
+        block = (local >= t * T) & (local < (t + 1) * T)
+        unit = jnp.where(local == sub + t * T, 1.0, 0.0)
+        for r in range(t, n):
+            tiles[r] = jnp.where(block, unit if r == t else 0.0, tiles[r])
         pivots = []
-        for i in range(T):
-            j = t * T + i
-            pivot = row_of(cols[i][t], i)
-            inv = 1.0 / pivot
-            pivots.append(pivot)
-            here = local == j
-            row = jnp.where(here, 1.0, row_of(tiles[t], i)) * inv
-            follow = [row_of(cols[m][t], i) * inv for m in range(i + 1, T)]
+        for i in range(0, T, 2):
+            a = row_of(cols[i][t], i)
+            b = row_of(cols[i][t], i + 1)
+            c = row_of(cols[i + 1][t], i + 1)
+            det = a * c - b * b
+            inv0 = 1.0 / a
+            inv1 = a * (1.0 / det)
+            ratio = b * inv0
+            pivots += [a, det * inv0]
+            row0, row1 = row_of(tiles[t], i), row_of(tiles[t], i + 1)
+            f0 = row0 * inv0
+            f1 = (row1 - ratio * row0) * inv1
+            follow = []
+            for m in range(i + 2, T):
+                u0, u1 = row_of(cols[m][t], i), row_of(cols[m][t], i + 1)
+                follow.append((u0 * inv0, (u1 - ratio * u0) * inv1))
             for r in range(t, n):
-                c = cols[i][r]
+                c0 = cols[i][r]
+                c1 = cols[i + 1][r] - ratio * c0
                 if r == t:
-                    c = jnp.where(sub > i, c, 0.0)
-                    keep = jnp.where(here & (sub > i), 0.0, tiles[r])
-                    keep = jnp.where(here & (sub == i), 1.0, keep)
-                else:
-                    keep = jnp.where(here, 0.0, tiles[r])
-                tiles[r] = keep - c * row
-                for m in range(i + 1, T):
-                    cols[m][r] = cols[m][r] - c * follow[m - i - 1]
+                    c0 = jnp.where(sub > i, c0, 0.0)
+                    c1 = jnp.where(sub > i + 1, c1, 0.0)
+                tiles[r] = (tiles[r] - c0 * f0) - c1 * f1
+                for m in range(i + 2, T):
+                    h0, h1 = follow[m - i - 2]
+                    cols[m][r] = (cols[m][r] - c0 * h0) - c1 * h1
         d = pivots[0]
         for i in range(1, T):
             d = jnp.where(sub == i, pivots[i], d)
@@ -116,20 +128,25 @@
                 tile = part if w == 0 else jnp.where(lane >= w * B, part, tile)
             tiles.append(tile)
         inv = jnp.concatenate(inverse_factors(tiles, lane), axis=0)
-        diag = jnp.concatenate([jnp.where(lane_b // B == w, inv, 0.0) for w in range(nwin)], axis=0)
-        rows = X[k]
-        q = dot(diag[:, : nwin * B], rows, HI)
         lane_q = lax.broadcasted_iota(jnp.int32, (B, 256), 1)
         inside = (lane_q >= k * B) & (lane_q < (k + 1) * B)
+        group = lane_b // B
         qs = []
         for w in range(nwin):
-            shift = (at - w * B) % 128
-            moved = jnp.where(lane_b // B == w, inv, 0.0)
-            if shift:
-                moved = pltpu.roll(moved, shift, 1)
-            zero = jnp.zeros((B, 128), F32)
-            wide = jnp.concatenate([moved, zero] if half == 0 else [zero, moved], axis=1)
-            qw = jnp.where(inside, wide, q[w * B : (w + 1) * B])
+            spread = jnp.concatenate(
+                [
+                    jnp.take_along_axis(inv[t * T : (t + 1) * T], w * B + lane % B, axis=1)
+                    for t in range(B // T)
+                ],
+                axis=0,
+            )
+            i1, i2, i3 = [piece.astype(F32) for piece in split3(spread)]
+            first = jnp.where(group < 3, i1, i2)
+            last = jnp.where(group == 0, i2, i3)
+            r1, r2, r3 = split3(X[k, w * B : (w + 1) * B, :])
+            left = jnp.concatenate([first, last], axis=1).astype(BF16)[:, : 6 * B]
+            qw = dot(left, jnp.concatenate([r1, r2, r3, r1, r2, r1], axis=0))
+            qw = jnp.where(inside, jnp.concatenate([spread, spread], axis=1), qw)
             qs.append(qw)
             X[k, w * B : (w + 1) * B, :] = jnp.where(lane_q < (k + 1) * B, qw, 0.0)
         if k + 1 == nb:
@@ -165,9 +182,9 @@
             col = columns[:slots, z * 8 + w : z * 8 + w + 1]
             parts.append(y.astype(F32) * col)
         weighted = jnp.concatenate(parts, axis=0)
-        hi, mid, lo = split3(weighted)
+        hi, mid, _ = split3(weighted)
         y = Y[w].T
-        return dot(y, hi) + (dot(y, mid) + dot(y, lo))
+        return dot(y, hi) + dot(y, mid)
 
     factor_body(nwin, gram, X)
     s = None
@@ -200,13 +217,12 @@
     )(g, scale, pltpu.with_memory_space_constraint(flat, pltpu.HBM))
 
 
-def pick_kernel(cells_ref, counts_ref, precision_ref, field_ref, out_ref, near, row_scr, sem):
+def pick_kernel(cells_ref, counts_ref, lanes_ref, precision_ref, field_ref, out_ref, near, row_scr, sem):
     nwin, slots = cells_ref.shape
     width = field_ref.shape[2]
 
     def copy_of(w, k):
-        offset = lax.rem(cells_ref[w, k], width)
-        first = pl.multiple_of((offset // 16) * 16, 16)
+        first = pl.multiple_of(jnp.bitwise_and(cells_ref[w, k], width - 16), 16)
         return pltpu.make_async_copy(field_ref.at[w, 0, pl.ds(first, 16), :], near.at[w * slots + k], sem)
 
     for w in range(nwin):
@@ -221,15 +237,13 @@
     low = (live - high.astype(F32)).astype(BF16)
     tail = jnp.concatenate([high, low], axis=1)
     pltpu.make_async_copy(near, near, sem).wait()
-    sub = lax.broadcasted_iota(jnp.int32, (16, 256), 0)
-    rows = []
+    spot = lax.broadcasted_iota(jnp.int32, (slots * 16, slots), 0)
+    slot = lax.broadcasted_iota(jnp.int32, (slots * 16, slots), 1)
     for w in range(nwin):
-        for k in range(slots):
-            within = lax.rem(cells_ref[w, k], 16)
-            tile = near[w * slots + k].astype(F32)
-            rows.append(jnp.sum(jnp.where(sub == within, tile, 0.0), axis=0, keepdims=True))
-    for w in range(nwin):
-        block = jnp.concatenate(rows[w * slots : (w + 1) * slots], axis=0).astype(BF16)
+        within = jnp.bitwise_and(lanes_ref[w : w + 1, :], 15)
+        chosen = jnp.where(spot == slot * 16 + within, 1.0, 0.0).astype(BF16)
+        tiles = near[w * slots : (w + 1) * slots].reshape(slots * 16, near.shape[2])
+        block = dot_tn(chosen, tiles).astype(BF16)
         for z in range(out_ref.shape[0]):
             out_ref[z, w * slots : (w + 1) * slots, :] = block
     for z in range(out_ref.shape[0]):
@@ -241,7 +255,7 @@
     members = anomalies.shape[3]
     return pl.pallas_call(
         pick_kernel,
-        in_specs=[SCALARS, SCALARS, WHOLE, pl.BlockSpec(memory_space=pltpu.HBM)],
+        in_specs=[SCALARS, SCALARS, WHOLE, WHOLE, pl.BlockSpec(memory_space=pltpu.HBM)],
         out_specs=WHOLE,
         out_shape=jax.ShapeDtypeStruct((copies, nwin * slots + 8, members), BF16),
         scratch_shapes=[
@@ -250,7 +264,7 @@
             pltpu.SemaphoreType.DMA,
         ],
         name="pick",
-    )(obs_cells, obs_counts, obs_precision, pltpu.with_memory_space_constraint(anomalies, pltpu.HBM))
+    )(obs_cells, obs_counts, obs_cells, obs_precision, pltpu.with_memory_space_constraint(anomalies, pltpu.HBM))
 
 
 def identity_bf16(n):

time: 68 us -> 65 us (0.956)
  Pallas kernels: 25.3 us -> 22.5 us
    pallas_call x1, Pallas kernels: 15 us -> 12.5 us  [factor_call(): pl.pallas_call(factor_kernel, in_specs=[WHOLE, SCALARS, pl.BlockSpec(memo...]
where the time goes in v3:
time: 65 us; the launch traced here: 64.8 us
  waiting for transfers between devices  24.5 us (38%)
  Pallas kernels  22.5 us (35%)
  starting transfers between devices  17.4 us (27%)
    all_to_all x1, waiting for transfers between devices, local(): lax.all_to_all(sent, 'cell', split_axis=0, concat_axis=0, tiled=True)  15.4 us
    pallas_call x1, Pallas kernels, factor_call(): pl.pallas_call(factor_kernel, in_specs=[WHOLE, SCALARS, pl.BlockSpec(memo...  12.5 us
    ppermute x7, waiting for transfers between devices, from_after(): lax.ppermute(array, axis, [(i, (i - shift) % count) for i in range(count)])  9.16 us
    ppermute x7, starting transfers between devices, from_after(): lax.ppermute(array, axis, [(i, (i - shift) % count) for i in range(count)])  8.97 us
    all_to_all x1, starting transfers between devices, local(): lax.all_to_all(sent, 'cell', split_axis=0, concat_axis=0, tiled=True)  8.48 us
    pallas_call x1, Pallas kernels, apply_call(): pl.pallas_call(apply_kernel, in_specs=[WHOLE] * 5, out_specs=pl.BlockSpec...  4.83 us
    pallas_call x1, Pallas kernels, pick_call(): pl.pallas_call(pick_kernel, in_specs=[SCALARS, SCALARS, WHOLE, WHOLE, pl....  3.13 us
    pallas_call x3, Pallas kernels, simple_call(): pl.pallas_call(kernel, in_specs=[WHOLE] * len(args), out_specs=jax.tree.m...  2.13 us
  transfers between devices with their start and end apart: 8, of which 7 were waited for; matrix products, arithmetic and copies ran while one was open for 0% of the time, Pallas kernels for 1%

profile of v3, /device:TPU:6, one launch (start us, length us, event | category | flops | bytes accessed | tf_op | source)
XLA Modules:
  0.0 64.8 jit_solution(16328288414810094557)
XLA Ops:
  0.0 0.0 copy-start
  0.0 3.1 %pick.1 = bf16[8,104,256]{2,1,0:T(8,128)(2,1)} custom-call(s32[3,32]{1,0:T(4,128)} %lanes_ref.1, s32[3]{0:T(128)} %bitcast.4, s32[3,32]{1,0:T(4,128)} %lanes_ref.1, f32[3,32]{1,0:T(4,128)} %precision_ref.1, bf16[3,2,2048,256]{3,2,1,0:T(8,128)(2,1)} %field_ref.1), custom_call_target="tpu_custom_call" | custom-call | tf_op jit(solution)/shard_map/pick/pallas_call | solution.py:256
  3.1 8.5 %all-to-all-start = ((bf16[8,104,256]{2,1,0:T(8,128)(2,1)}), bf16[8,104,256]{2,1,0:T(8,128)(2,1)S(1)}, u32[]{:S(2)}, u32[]{:S(2)}) async-start(bf16[8,104,256]{2,1,0:T(8,128)(2,1)} %pick.1), calls=%async_computation | async-start | bytes 851968 | tf_op jit(solution)/shard_map/all_to_all | solution.py:412
  11.6 0.0 copy-done
  11.6 15.4 %all-to-all-done.g_ref = bf16[8,104,256]{2,1,0:T(8,128)(2,1)S(1)} async-done(((bf16[8,104,256]{2,1,0:T(8,128)(2,1)}), bf16[8,104,256]{2,1,0:T(8,128)(2,1)S(1)}, u32[]{:S(2)}, u32[]{:S(2)}) %all-to-all-start) | async-done | bytes 426016 | tf_op jit(solution)/shard_map/all_to_all | solution.py:412
  27.0 12.5 %factor.1 = (f32[3,256,256]{2,1,0:T(8,128)S(1)}, bf16[320,128]{1,0:T(8,128)(2,1)S(1)}, bf16[3,4096,256]{2,1,0:T(8,128)(2,1)S(1)}) custom-call(bf16[8,104,256]{2,1,0:T(8,128)(2,1)S(1)} %all-to-all-done.g_ref, f32[3]{0:T(128)S(1)} %broadcast_multiply_fusion.scale_ref, bf16[3,4096,256]{2,1,0:T(8,128)(2,1)} %bitcast.3), custom_call_target="tpu_custom_call" | custom-call | tf_op jit(solution)/shard_map/factor/pallas_call | solution.py:201
  39.5 0.1 collective-permute-start
  39.6 1.3 %collective-permute-done.other_ref = bf16[320,128]{1,0:T(8,128)(2,1)S(1)} collective-permute-done((bf16[320,128]{1,0:T(8,128)(2,1)S(1)}, bf16[320,128]{1,0:T(8,128)(2,1)S(1)}, u32[]{:S(2)}, u32[]{:S(2)}) %collective-permute-start) | collective-permute-done | bytes 81952 | tf_op jit(solution)/shard_map/ppermute | solution.py:404
  40.8 0.3 pair.1.p0
  41.1 1.7 %collective-permute-start.3 = (bf16[320,128]{1,0:T(8,128)(2,1)S(1)}, bf16[320,128]{1,0:T(8,128)(2,1)S(1)}, u32[]{:S(2)}, u32[]{:S(2)}) collective-permute-start(bf16[320,128]{1,0:T(8,128)(2,1)S(1)} %pair.1.p0), channel_id=1, source_target_pairs={{0,16},{16,32},{32,48},{48,0},{1,17},{17,33},{33,49},{49,1},{2,18}... | collective-permute-start | bytes 245768 | tf_op jit(solution)/shard_map/ppermute | solution.py:404
  42.8 2.9 %collective-permute-start.2 = (bf16[320,128]{1,0:T(8,128)(2,1)S(1)}, bf16[320,128]{1,0:T(8,128)(2,1)S(1)}, u32[]{:S(2)}, u32[]{:S(2)}) collective-permute-start(bf16[320,128]{1,0:T(8,128)(2,1)S(1)} %pair.1.p0), channel_id=1, source_target_pairs={{0,32},{16,48},{32,0},{48,16},{1,33},{17,49},{33,1},{49,17},{2,34}... | collective-permute-start | bytes 245768 | tf_op jit(solution)/shard_map/ppermute | solution.py:404
  45.7 1.3 %collective-permute-start.1 = (bf16[320,128]{1,0:T(8,128)(2,1)S(1)}, bf16[320,128]{1,0:T(8,128)(2,1)S(1)}, u32[]{:S(2)}, u32[]{:S(2)}) collective-permute-start(bf16[320,128]{1,0:T(8,128)(2,1)S(1)} %pair.1.p0), channel_id=1, source_target_pairs={{0,48},{16,0},{32,16},{48,32},{1,49},{17,1},{33,17},{49,33},{2,50}... | collective-permute-start | bytes 245768 | tf_op jit(solution)/shard_map/ppermute | solution.py:404
  47.0 0.0 collective-permute-done.3.p3
  47.0 2.9 %collective-permute-done.2.p2 = bf16[320,128]{1,0:T(8,128)(2,1)S(1)} collective-permute-done((bf16[320,128]{1,0:T(8,128)(2,1)S(1)}, bf16[320,128]{1,0:T(8,128)(2,1)S(1)}, u32[]{:S(2)}, u32[]{:S(2)}) %collective-permute-start.2) | collective-permute-done | bytes 81952 | tf_op jit(solution)/shard_map/ppermute | solution.py:404
  49.9 0.2 collective-permute-done.1.p1
  50.1 1.0 %ring.1 = (bf16[320,128]{1,0:T(8,128)(2,1)S(1)}, f32[256,256]{1,0:T(8,128)S(1)}) custom-call(bf16[320,128]{1,0:T(8,128)(2,1)S(1)} %pair.1.p0, bf16[320,128]{1,0:T(8,128)(2,1)S(1)} %collective-permute-done.1.p1, bf16[320,128]{1,0:T(8,128)(2,1)S(1)} %collective-permute-done.2.p2, bf16[320,128]{1,0:T(8,128)(2,1)S(1)} %collective-permute-done.3.p3), custom_call_target="tpu_custom_call" | custom-call | tf_op jit(solution)/shard_map/ring/pallas_call | solution.py:391
  51.1 0.6 collective-permute-start.6
  51.7 2.4 %collective-permute-start.5 = (bf16[320,128]{1,0:T(8,128)(2,1)S(1)}, bf16[320,128]{1,0:T(8,128)(2,1)S(1)}, u32[]{:S(2)}, u32[]{:S(2)}) collective-permute-start(bf16[320,128]{1,0:T(8,128)(2,1)S(1)} %get-tuple-element.11), channel_id=1, source_target_pairs={{0,128},{64,192},{128,0},{192,64},{1,129},{65,193},{129,1},{193,65... | collective-permute-start | bytes 245768 | tf_op jit(solution)/shard_map/ppermute | solution.py:404
  54.1 0.0 collective-permute-start.4
  54.1 0.8 %inner.1.inner_ref = f32[3,256,256]{2,1,0:T(8,128)S(1)} custom-call(f32[256,256]{1,0:T(8,128)S(1)} %get-tuple-element.12.later_ref, bf16[320,128]{1,0:T(8,128)(2,1)S(1)} %collective-permute-done.other_ref, f32[3,256,256]{2,1,0:T(8,128)S(1)} %get-tuple-element.13.part_ref), custom_call_target="tpu_custom_call" | custom-call | tf_op jit(solution)/shard_map/inner/pallas_call | solution.py:391
  55.0 0.7 %collective-permute-done.6.p3 = bf16[320,128]{1,0:T(8,128)(2,1)S(1)} collective-permute-done((bf16[320,128]{1,0:T(8,128)(2,1)S(1)}, bf16[320,128]{1,0:T(8,128)(2,1)S(1)}, u32[]{:S(2)}, u32[]{:S(2)}) %collective-permute-start.6) | collective-permute-done | bytes 81952 | tf_op jit(solution)/shard_map/ppermute | solution.py:404
  55.7 2.6 %collective-permute-done.5.p2 = bf16[320,128]{1,0:T(8,128)(2,1)S(1)} collective-permute-done((bf16[320,128]{1,0:T(8,128)(2,1)S(1)}, bf16[320,128]{1,0:T(8,128)(2,1)S(1)}, u32[]{:S(2)}, u32[]{:S(2)}) %collective-permute-start.5) | collective-permute-done | bytes 81952 | tf_op jit(solution)/shard_map/ppermute | solution.py:404
  58.2 1.5 %collective-permute-done.4.p1 = bf16[320,128]{1,0:T(8,128)(2,1)S(1)} collective-permute-done((bf16[320,128]{1,0:T(8,128)(2,1)S(1)}, bf16[320,128]{1,0:T(8,128)(2,1)S(1)}, u32[]{:S(2)}, u32[]{:S(2)}) %collective-permute-start.4) | collective-permute-done | bytes 81952 | tf_op jit(solution)/shard_map/ppermute | solution.py:404
  59.8 4.8 %apply.1 = bf16[3,4096,256]{2,1,0:T(8,128)(2,1)} custom-call(bf16[320,128]{1,0:T(8,128)(2,1)S(1)} %collective-permute-done.4.p1, bf16[320,128]{1,0:T(8,128)(2,1)S(1)} %collective-permute-done.5.p2, bf16[320,128]{1,0:T(8,128)(2,1)S(1)} %collective-permute-done.6.p3, f32[3,256,256]{2,1,0:T(8,128)S(1)} %inner.1.inner_ref, ...), custom_call_target="tpu_custom_call" | custom-call | tf_op jit(solution)/shard_map/apply/pallas_call | solution.py:374
  (1 shorter events, 0.0 us)
Async XLA Ops:
  0.0 11.6 %copy-start = (f32[3]{0:T(128)S(1)}, f32[3]{0:T(128)}, u32[]{:S(2)}) copy-start(f32[3]{0:T(128)} %param.9) | copy-start | bytes 40
  3.1 23.9 %all-to-all-start = ((bf16[8,104,256]{2,1,0:T(8,128)(2,1)}), bf16[8,104,256]{2,1,0:T(8,128)(2,1)S(1)}, u32[]{:S(2)}, u32[]{:S(2)}) async-start(bf16[8,104,256]{2,1,0:T(8,128)(2,1)} %pick.1), calls=%async_computation | async-start | bytes 851968 | tf_op jit(solution)/shard_map/all_to_all | solution.py:412
  39.5 1.4 %collective-permute-start = (bf16[320,128]{1,0:T(8,128)(2,1)S(1)}, bf16[320,128]{1,0:T(8,128)(2,1)S(1)}, u32[]{:S(2)}, u32[]{:S(2)}) collective-permute-start(bf16[320,128]{1,0:T(8,128)(2,1)S(1)} %get-tuple-element.10.mine_ref), channel_id=1, source_target_pairs={{0,8},{8,0},{1,9},{9,1},{2,10},{10,2},{3,11},{11,3},{4,12},{12,4},... | collective-permute-start | bytes 245768 | tf_op jit(solution)/shard_map/ppermute | solution.py:404
  41.1 5.9 %collective-permute-start.3 = (bf16[320,128]{1,0:T(8,128)(2,1)S(1)}, bf16[320,128]{1,0:T(8,128)(2,1)S(1)}, u32[]{:S(2)}, u32[]{:S(2)}) collective-permute-start(bf16[320,128]{1,0:T(8,128)(2,1)S(1)} %pair.1.p0), channel_id=1, source_target_pairs={{0,16},{16,32},{32,48},{48,0},{1,17},{17,33},{33,49},{49,1},{2,18}... | collective-permute-start | bytes 245768 | tf_op jit(solution)/shard_map/ppermute | solution.py:404
  42.8 7.1 %collective-permute-start.2 = (bf16[320,128]{1,0:T(8,128)(2,1)S(1)}, bf16[320,128]{1,0:T(8,128)(2,1)S(1)}, u32[]{:S(2)}, u32[]{:S(2)}) collective-permute-start(bf16[320,128]{1,0:T(8,128)(2,1)S(1)} %pair.1.p0), channel_id=1, source_target_pairs={{0,32},{16,48},{32,0},{48,16},{1,33},{17,49},{33,1},{49,17},{2,34}... | collective-permute-start | bytes 245768 | tf_op jit(solution)/shard_map/ppermute | solution.py:404
  45.7 4.4 %collective-permute-start.1 = (bf16[320,128]{1,0:T(8,128)(2,1)S(1)}, bf16[320,128]{1,0:T(8,128)(2,1)S(1)}, u32[]{:S(2)}, u32[]{:S(2)}) collective-permute-start(bf16[320,128]{1,0:T(8,128)(2,1)S(1)} %pair.1.p0), channel_id=1, source_target_pairs={{0,48},{16,0},{32,16},{48,32},{1,49},{17,1},{33,17},{49,33},{2,50}... | collective-permute-start | bytes 245768 | tf_op jit(solution)/shard_map/ppermute | solution.py:404
  51.1 4.5 %collective-permute-start.6 = (bf16[320,128]{1,0:T(8,128)(2,1)S(1)}, bf16[320,128]{1,0:T(8,128)(2,1)S(1)}, u32[]{:S(2)}, u32[]{:S(2)}) collective-permute-start(bf16[320,128]{1,0:T(8,128)(2,1)S(1)} %get-tuple-element.11), channel_id=1, source_target_pairs={{0,64},{64,128},{128,192},{192,0},{1,65},{65,129},{129,193},{193,1... | collective-permute-start | bytes 245768 | tf_op jit(solution)/shard_map/ppermute | solution.py:404
  51.7 6.5 %collective-permute-start.5 = (bf16[320,128]{1,0:T(8,128)(2,1)S(1)}, bf16[320,128]{1,0:T(8,128)(2,1)S(1)}, u32[]{:S(2)}, u32[]{:S(2)}) collective-permute-start(bf16[320,128]{1,0:T(8,128)(2,1)S(1)} %get-tuple-element.11), channel_id=1, source_target_pairs={{0,128},{64,192},{128,0},{192,64},{1,129},{65,193},{129,1},{193,65... | collective-permute-start | bytes 245768 | tf_op jit(solution)/shard_map/ppermute | solution.py:404
  54.1 5.7 %collective-permute-start.4 = (bf16[320,128]{1,0:T(8,128)(2,1)S(1)}, bf16[320,128]{1,0:T(8,128)(2,1)S(1)}, u32[]{:S(2)}, u32[]{:S(2)}) collective-permute-start(bf16[320,128]{1,0:T(8,128)(2,1)S(1)} %get-tuple-element.11), channel_id=1, source_target_pairs={{0,192},{64,0},{128,64},{192,128},{1,193},{65,1},{129,65},{193,129... | collective-permute-start | bytes 245768 | tf_op jit(solution)/shard_map/ppermute | solution.py:404

commit v4 on v3

--- a/solution.py
+++ b/solution.py
@@ -44,6 +44,14 @@
     bh = b.astype(BF16)
     bl = (b - bh.astype(F32)).astype(BF16)
     return dot(ah, bh) + (dot(ah, bl) + dot(al, bh))
+
+
+def dot_nt_x3(a, b):
+    ah = a.astype(BF16)
+    al = (a - ah.astype(F32)).astype(BF16)
+    bh = b.astype(BF16)
+    bl = (b - bh.astype(F32)).astype(BF16)
+    return dot_nt(ah, bh) + (dot_nt(ah, bl) + dot_nt(al, bh))
 
 
 def row_of(tile, i):
@@ -328,7 +336,7 @@
         before[...] = dot_x3(later_ref[...], unpack(other_ref[...].astype(F32)))
 
     for w in range(part_ref.shape[0]):
-        out_ref[w] = dot_x3(before[...], part_ref[w])
+        out_ref[w] = dot_x3(before[...], part_ref[w]).T
 
 
 def apply_kernel(p1, p2, p3, inner_ref, field_ref, out_ref, q, later, result, sems):
@@ -355,7 +363,7 @@
     nwin, rows, _ = field_ref.shape
     copies = []
     for w in range(nwin):
-        weights = dot_x3(later[...], inner_ref[w]).T.astype(BF16)
+        weights = dot_nt_x3(inner_ref[w], later[...]).astype(BF16)
         for half in range(STEPS):
             span = pl.ds(half * (rows // STEPS), rows // STEPS)
             result[w, span, :] = dot(field_ref[w, span, :], weights).astype(BF16)
@@ -366,7 +374,7 @@
         copy.wait()
 
 
-STEPS = 2
+STEPS = 4
 
 
 def apply_call(pieces, inner, flat):

time: 65 us -> 64.6 us (level)
  transfers between devices with their start and end apart: 8 -> 8, of which waited for: 7 -> 7; matrix products, arithmetic and copies ran while one was open for 0% -> 0% of each run, Pallas kernels for 1% -> 2%
where the time goes in v4:
time: 64.6 us; the launch traced here: 64.3 us
  waiting for transfers between devices  24.4 us (38%)
  Pallas kernels  22.2 us (34%)
  starting transfers between devices  17.4 us (27%)
    all_to_all x1, waiting for transfers between devices, local(): lax.all_to_all(sent, 'cell', split_axis=0, concat_axis=0, tiled=True)  15.4 us
    pallas_call x1, Pallas kernels, factor_call(): pl.pallas_call(factor_kernel, in_specs=[WHOLE, SCALARS, pl.BlockSpec(memo...  12.5 us
    ppermute x7, waiting for transfers between devices, from_after(): lax.ppermute(array, axis, [(i, (i - shift) % count) for i in range(count)])  9.02 us
    ppermute x7, starting transfers between devices, from_after(): lax.ppermute(array, axis, [(i, (i - shift) % count) for i in range(count)])  8.97 us
    all_to_all x1, starting transfers between devices, local(): lax.all_to_all(sent, 'cell', split_axis=0, concat_axis=0, tiled=True)  8.48 us
    pallas_call x1, Pallas kernels, apply_call(): pl.pallas_call(apply_kernel, in_specs=[WHOLE] * 5, out_specs=pl.BlockSpec...  4.35 us
    pallas_call x1, Pallas kernels, pick_call(): pl.pallas_call(pick_kernel, in_specs=[SCALARS, SCALARS, WHOLE, WHOLE, pl....  3.13 us
    pallas_call x3, Pallas kernels, simple_call(): pl.pallas_call(kernel, in_specs=[WHOLE] * len(args), out_specs=jax.tree.m...  2.27 us
  transfers between devices with their start and end apart: 8, of which 7 were waited for; matrix products, arithmetic and copies ran while one was open for 0% of the time, Pallas kernels for 2%

profile of v4, /device:TPU:6, one launch (start us, length us, event | category | flops | bytes accessed | tf_op | source)
XLA Modules:
  0.0 64.3 jit_solution(15507907086998728979)
XLA Ops:
  0.0 0.0 copy-start
  0.0 3.1 %pick.1 = bf16[8,104,256]{2,1,0:T(8,128)(2,1)} custom-call(s32[3,32]{1,0:T(4,128)} %lanes_ref.1, s32[3]{0:T(128)} %bitcast.4, s32[3,32]{1,0:T(4,128)} %lanes_ref.1, f32[3,32]{1,0:T(4,128)} %precision_ref.1, bf16[3,2,2048,256]{3,2,1,0:T(8,128)(2,1)} %field_ref.1), custom_call_target="tpu_custom_call" | custom-call | tf_op jit(solution)/shard_map/pick/pallas_call | solution.py:264
  3.1 8.5 %all-to-all-start = ((bf16[8,104,256]{2,1,0:T(8,128)(2,1)}), bf16[8,104,256]{2,1,0:T(8,128)(2,1)S(1)}, u32[]{:S(2)}, u32[]{:S(2)}) async-start(bf16[8,104,256]{2,1,0:T(8,128)(2,1)} %pick.1), calls=%async_computation | async-start | bytes 851968 | tf_op jit(solution)/shard_map/all_to_all | solution.py:420
  11.6 0.0 copy-done
  11.6 15.4 %all-to-all-done.g_ref = bf16[8,104,256]{2,1,0:T(8,128)(2,1)S(1)} async-done(((bf16[8,104,256]{2,1,0:T(8,128)(2,1)}), bf16[8,104,256]{2,1,0:T(8,128)(2,1)S(1)}, u32[]{:S(2)}, u32[]{:S(2)}) %all-to-all-start) | async-done | bytes 426016 | tf_op jit(solution)/shard_map/all_to_all | solution.py:420
  27.0 12.5 %factor.1 = (f32[3,256,256]{2,1,0:T(8,128)S(1)}, bf16[320,128]{1,0:T(8,128)(2,1)S(1)}, bf16[3,4096,256]{2,1,0:T(8,128)(2,1)S(1)}) custom-call(bf16[8,104,256]{2,1,0:T(8,128)(2,1)S(1)} %all-to-all-done.g_ref, f32[3]{0:T(128)S(1)} %broadcast_multiply_fusion.scale_ref, bf16[3,4096,256]{2,1,0:T(8,128)(2,1)} %bitcast.3), custom_call_target="tpu_custom_call" | custom-call | tf_op jit(solution)/shard_map/factor/pallas_call | solution.py:209
  39.5 0.1 collective-permute-start
  39.6 1.3 %collective-permute-done.other_ref = bf16[320,128]{1,0:T(8,128)(2,1)S(1)} collective-permute-done((bf16[320,128]{1,0:T(8,128)(2,1)S(1)}, bf16[320,128]{1,0:T(8,128)(2,1)S(1)}, u32[]{:S(2)}, u32[]{:S(2)}) %collective-permute-start) | collective-permute-done | bytes 81952 | tf_op jit(solution)/shard_map/ppermute | solution.py:412
  40.8 0.3 pair.1.p0
  41.1 1.7 %collective-permute-start.3 = (bf16[320,128]{1,0:T(8,128)(2,1)S(1)}, bf16[320,128]{1,0:T(8,128)(2,1)S(1)}, u32[]{:S(2)}, u32[]{:S(2)}) collective-permute-start(bf16[320,128]{1,0:T(8,128)(2,1)S(1)} %pair.1.p0), channel_id=1, source_target_pairs={{0,16},{16,32},{32,48},{48,0},{1,17},{17,33},{33,49},{49,1},{2,18}... | collective-permute-start | bytes 245768 | tf_op jit(solution)/shard_map/ppermute | solution.py:412
  42.8 2.9 %collective-permute-start.2 = (bf16[320,128]{1,0:T(8,128)(2,1)S(1)}, bf16[320,128]{1,0:T(8,128)(2,1)S(1)}, u32[]{:S(2)}, u32[]{:S(2)}) collective-permute-start(bf16[320,128]{1,0:T(8,128)(2,1)S(1)} %pair.1.p0), channel_id=1, source_target_pairs={{0,32},{16,48},{32,0},{48,16},{1,33},{17,49},{33,1},{49,17},{2,34}... | collective-permute-start | bytes 245768 | tf_op jit(solution)/shard_map/ppermute | solution.py:412
  45.7 1.3 %collective-permute-start.1 = (bf16[320,128]{1,0:T(8,128)(2,1)S(1)}, bf16[320,128]{1,0:T(8,128)(2,1)S(1)}, u32[]{:S(2)}, u32[]{:S(2)}) collective-permute-start(bf16[320,128]{1,0:T(8,128)(2,1)S(1)} %pair.1.p0), channel_id=1, source_target_pairs={{0,48},{16,0},{32,16},{48,32},{1,49},{17,1},{33,17},{49,33},{2,50}... | collective-permute-start | bytes 245768 | tf_op jit(solution)/shard_map/ppermute | solution.py:412
  47.0 0.0 collective-permute-done.3.p3
  47.0 2.9 %collective-permute-done.2.p2 = bf16[320,128]{1,0:T(8,128)(2,1)S(1)} collective-permute-done((bf16[320,128]{1,0:T(8,128)(2,1)S(1)}, bf16[320,128]{1,0:T(8,128)(2,1)S(1)}, u32[]{:S(2)}, u32[]{:S(2)}) %collective-permute-start.2) | collective-permute-done | bytes 81952 | tf_op jit(solution)/shard_map/ppermute | solution.py:412
  49.9 0.2 collective-permute-done.1.p1
  50.1 1.0 %ring.1 = (bf16[320,128]{1,0:T(8,128)(2,1)S(1)}, f32[256,256]{1,0:T(8,128)S(1)}) custom-call(bf16[320,128]{1,0:T(8,128)(2,1)S(1)} %pair.1.p0, bf16[320,128]{1,0:T(8,128)(2,1)S(1)} %collective-permute-done.1.p1, bf16[320,128]{1,0:T(8,128)(2,1)S(1)} %collective-permute-done.2.p2, bf16[320,128]{1,0:T(8,128)(2,1)S(1)} %collective-permute-done.3.p3), custom_call_target="tpu_custom_call" | custom-call | tf_op jit(solution)/shard_map/ring/pallas_call | solution.py:399
  51.1 0.6 collective-permute-start.6
  51.7 2.4 %collective-permute-start.5 = (bf16[320,128]{1,0:T(8,128)(2,1)S(1)}, bf16[320,128]{1,0:T(8,128)(2,1)S(1)}, u32[]{:S(2)}, u32[]{:S(2)}) collective-permute-start(bf16[320,128]{1,0:T(8,128)(2,1)S(1)} %get-tuple-element.11), channel_id=1, source_target_pairs={{0,128},{64,192},{128,0},{192,64},{1,129},{65,193},{129,1},{193,65... | collective-permute-start | bytes 245768 | tf_op jit(solution)/shard_map/ppermute | solution.py:412
  54.1 0.0 collective-permute-start.4
  54.1 1.0 %inner.1.inner_ref = f32[3,256,256]{2,1,0:T(8,128)S(1)} custom-call(f32[256,256]{1,0:T(8,128)S(1)} %get-tuple-element.12.later_ref, bf16[320,128]{1,0:T(8,128)(2,1)S(1)} %collective-permute-done.other_ref, f32[3,256,256]{2,1,0:T(8,128)S(1)} %get-tuple-element.13.part_ref), custom_call_target="tpu_custom_call" | custom-call | tf_op jit(solution)/shard_map/inner/pallas_call | solution.py:399
  55.1 0.6 collective-permute-done.6.p3
  55.7 2.6 %collective-permute-done.5.p2 = bf16[320,128]{1,0:T(8,128)(2,1)S(1)} collective-permute-done((bf16[320,128]{1,0:T(8,128)(2,1)S(1)}, bf16[320,128]{1,0:T(8,128)(2,1)S(1)}, u32[]{:S(2)}, u32[]{:S(2)}) %collective-permute-start.5) | collective-permute-done | bytes 81952 | tf_op jit(solution)/shard_map/ppermute | solution.py:412
  58.2 1.5 %collective-permute-done.4.p1 = bf16[320,128]{1,0:T(8,128)(2,1)S(1)} collective-permute-done((bf16[320,128]{1,0:T(8,128)(2,1)S(1)}, bf16[320,128]{1,0:T(8,128)(2,1)S(1)}, u32[]{:S(2)}, u32[]{:S(2)}) %collective-permute-start.4) | collective-permute-done | bytes 81952 | tf_op jit(solution)/shard_map/ppermute | solution.py:412
  59.8 4.4 %apply.1 = bf16[3,4096,256]{2,1,0:T(8,128)(2,1)} custom-call(bf16[320,128]{1,0:T(8,128)(2,1)S(1)} %collective-permute-done.4.p1, bf16[320,128]{1,0:T(8,128)(2,1)S(1)} %collective-permute-done.5.p2, bf16[320,128]{1,0:T(8,128)(2,1)S(1)} %collective-permute-done.6.p3, f32[3,256,256]{2,1,0:T(8,128)S(1)} %inner.1.inner_ref, ...), custom_call_target="tpu_custom_call" | custom-call | tf_op jit(solution)/shard_map/apply/pallas_call | solution.py:382
  (1 shorter events, 0.0 us)
Async XLA Ops:
  0.0 11.6 %copy-start = (f32[3]{0:T(128)S(1)}, f32[3]{0:T(128)}, u32[]{:S(2)}) copy-start(f32[3]{0:T(128)} %param.9) | copy-start | bytes 40
  3.1 23.9 %all-to-all-start = ((bf16[8,104,256]{2,1,0:T(8,128)(2,1)}), bf16[8,104,256]{2,1,0:T(8,128)(2,1)S(1)}, u32[]{:S(2)}, u32[]{:S(2)}) async-start(bf16[8,104,256]{2,1,0:T(8,128)(2,1)} %pick.1), calls=%async_computation | async-start | bytes 851968 | tf_op jit(solution)/shard_map/all_to_all | solution.py:420
  39.5 1.4 %collective-permute-start = (bf16[320,128]{1,0:T(8,128)(2,1)S(1)}, bf16[320,128]{1,0:T(8,128)(2,1)S(1)}, u32[]{:S(2)}, u32[]{:S(2)}) collective-permute-start(bf16[320,128]{1,0:T(8,128)(2,1)S(1)} %get-tuple-element.10.mine_ref), channel_id=1, source_target_pairs={{0,8},{8,0},{1,9},{9,1},{2,10},{10,2},{3,11},{11,3},{4,12},{12,4},... | collective-permute-start | bytes 245768 | tf_op jit(solution)/shard_map/ppermute | solution.py:412
  41.1 5.9 %collective-permute-start.3 = (bf16[320,128]{1,0:T(8,128)(2,1)S(1)}, bf16[320,128]{1,0:T(8,128)(2,1)S(1)}, u32[]{:S(2)}, u32[]{:S(2)}) collective-permute-start(bf16[320,128]{1,0:T(8,128)(2,1)S(1)} %pair.1.p0), channel_id=1, source_target_pairs={{0,16},{16,32},{32,48},{48,0},{1,17},{17,33},{33,49},{49,1},{2,18}... | collective-permute-start | bytes 245768 | tf_op jit(solution)/shard_map/ppermute | solution.py:412
  42.8 7.1 %collective-permute-start.2 = (bf16[320,128]{1,0:T(8,128)(2,1)S(1)}, bf16[320,128]{1,0:T(8,128)(2,1)S(1)}, u32[]{:S(2)}, u32[]{:S(2)}) collective-permute-start(bf16[320,128]{1,0:T(8,128)(2,1)S(1)} %pair.1.p0), channel_id=1, source_target_pairs={{0,32},{16,48},{32,0},{48,16},{1,33},{17,49},{33,1},{49,17},{2,34}... | collective-permute-start | bytes 245768 | tf_op jit(solution)/shard_map/ppermute | solution.py:412
  45.7 4.4 %collective-permute-start.1 = (bf16[320,128]{1,0:T(8,128)(2,1)S(1)}, bf16[320,128]{1,0:T(8,128)(2,1)S(1)}, u32[]{:S(2)}, u32[]{:S(2)}) collective-permute-start(bf16[320,128]{1,0:T(8,128)(2,1)S(1)} %pair.1.p0), channel_id=1, source_target_pairs={{0,48},{16,0},{32,16},{48,32},{1,49},{17,1},{33,17},{49,33},{2,50}... | collective-permute-start | bytes 245768 | tf_op jit(solution)/shard_map/ppermute | solution.py:412
  51.1 4.5 %collective-permute-start.6 = (bf16[320,128]{1,0:T(8,128)(2,1)S(1)}, bf16[320,128]{1,0:T(8,128)(2,1)S(1)}, u32[]{:S(2)}, u32[]{:S(2)}) collective-permute-start(bf16[320,128]{1,0:T(8,128)(2,1)S(1)} %get-tuple-element.11), channel_id=1, source_target_pairs={{0,64},{64,128},{128,192},{192,0},{1,65},{65,129},{129,193},{193,1... | collective-permute-start | bytes 245768 | tf_op jit(solution)/shard_map/ppermute | solution.py:412
  51.7 6.5 %collective-permute-start.5 = (bf16[320,128]{1,0:T(8,128)(2,1)S(1)}, bf16[320,128]{1,0:T(8,128)(2,1)S(1)}, u32[]{:S(2)}, u32[]{:S(2)}) collective-permute-start(bf16[320,128]{1,0:T(8,128)(2,1)S(1)} %get-tuple-element.11), channel_id=1, source_target_pairs={{0,128},{64,192},{128,0},{192,64},{1,129},{65,193},{129,1},{193,65... | collective-permute-start | bytes 245768 | tf_op jit(solution)/shard_map/ppermute | solution.py:412
  54.1 5.7 %collective-permute-start.4 = (bf16[320,128]{1,0:T(8,128)(2,1)S(1)}, bf16[320,128]{1,0:T(8,128)(2,1)S(1)}, u32[]{:S(2)}, u32[]{:S(2)}) collective-permute-start(bf16[320,128]{1,0:T(8,128)(2,1)S(1)} %get-tuple-element.11), channel_id=1, source_target_pairs={{0,192},{64,0},{128,64},{192,128},{1,193},{65,1},{129,65},{193,129... | collective-permute-start | bytes 245768 | tf_op jit(solution)/shard_map/ppermute | solution.py:412
